TPU v7x, 256 devices: a whole 4x4x8 slice. The times are simulated.
256 devices in a mesh: ma: 32 (over z, x_lo, core), bl: 8 (over y, x_hi).
Axes of the slice: x: 4 (x_hi: 2, x_lo: 2; x = x_hi * 2 + x_lo), y: 4, z: 8, core: 2. Of those that a mesh axis runs over, the one named last changes fastest.
Arguments:
- visibilities: bfloat16 [2, 16640, 8192], P(None, 'bl', 'ma'), may hold values from -6 to 6
- beam_blocks: bfloat16 [32, 2, 16640, 1000], P('ma', None, 'bl'), may hold values from -0.0625 to 0.0625
- feed_pairs: int32 [16640, 2], P('bl'), may hold values from 0 to 1023
- feed_gains: float32 [2, 1024], replicated, may hold values from -1.5 to 1.5
- m_order: int32 [32], replicated, may hold values from 0 to 31, each once
Outputs:
- sky_modes: float32 [2, 32, 1000], P(None, 'ma', 'bl')
All inputs are finite; a program needn't handle non-finite values.
Results may differ from a plain program's by a relative error of at most 0.0049.
Values may be sent and summed in bfloat16 or wider, within the bound.
No kernel may reach another device: no remote copies, remote signals or barrier semaphores. Data moves between devices by JAX's collectives and lax.ppermute only.
A program may use at most 64 MiB of HBM per device.

v0:
```python
import jax
import jax.numpy as jnp
from jax import lax
from jax.sharding import PartitionSpec as P

NT = 8192


def dft_weights(time_index, m_values):
    wrapped = jnp.mod(time_index[:, None] * m_values[None, :], NT).astype(jnp.float32)
    phases = wrapped * (2.0 * jnp.pi / NT)
    scale = 1.0 / jnp.sqrt(jnp.float32(NT))
    cos_part = (jnp.cos(phases) * scale).astype(jnp.bfloat16)
    sin_part = (jnp.sin(phases) * scale).astype(jnp.bfloat16)
    upper = jnp.concatenate([cos_part, -sin_part], axis=1)
    lower = jnp.concatenate([sin_part, cos_part], axis=1)
    return jnp.concatenate([upper, lower], axis=0)


def transform(visible, weights, count):
    stacked_in = jnp.concatenate([visible[0], visible[1]], axis=1)
    flat = jnp.dot(stacked_in, weights, preferred_element_type=jnp.float32)
    return jnp.stack([flat[:, :count], flat[:, count:]])


def per_device(visibilities, beam_blocks, feed_pairs, feed_gains, m_order):
    count = m_order.shape[0]
    m_values = m_order - count // 2
    turned = lax.all_to_all(visibilities, "ma", split_axis=1, concat_axis=2, tiled=True)
    time_index = jnp.arange(NT, dtype=jnp.int32)
    weights = dft_weights(time_index, m_values)
    spectra_all = transform(turned, weights, count).astype(jnp.bfloat16)
    owned = lax.all_to_all(spectra_all, "ma", split_axis=2, concat_axis=1, tiled=True)
    local_rows = feed_pairs.shape[0]
    feed_count = feed_gains.shape[1]
    both_feeds = jnp.concatenate([feed_pairs[:, 0], feed_pairs[:, 1]], axis=0)
    feed_iota = jnp.arange(feed_count, dtype=jnp.int32)
    one_hot = (both_feeds[:, None] == feed_iota[None, :]).astype(jnp.float32)
    picked = jnp.dot(
        one_hot,
        jnp.transpose(feed_gains),
        precision=lax.Precision.HIGHEST,
        preferred_element_type=jnp.float32,
    )
    a_re = picked[:local_rows, 0]
    a_im = picked[:local_rows, 1]
    b_re = picked[local_rows:, 0]
    b_im = picked[local_rows:, 1]
    factor_re = (a_re * b_re + a_im * b_im)[:, None]
    factor_im = (a_im * b_re - a_re * b_im)[:, None]
    spec_re = owned[0].astype(jnp.float32)
    spec_im = owned[1].astype(jnp.float32)
    weighted_re = (spec_re * factor_re - spec_im * factor_im).astype(jnp.bfloat16)
    weighted_im = (spec_re * factor_im + spec_im * factor_re).astype(jnp.bfloat16)
    row_real = jnp.concatenate([weighted_re, weighted_im], axis=0)
    row_imag = jnp.concatenate([weighted_im, -weighted_re], axis=0)
    vectors = jnp.transpose(jnp.stack([row_real, row_imag]), (2, 0, 1))
    local_modes = beam_blocks.shape[0]
    block_rows = beam_blocks.shape[2]
    width = beam_blocks.shape[3]
    flat_blocks = beam_blocks.reshape(local_modes, 2 * block_rows, width)
    partial_value = jnp.einsum(
        "mkc,mcl->kml", vectors, flat_blocks, preferred_element_type=jnp.float32
    )
    totals = lax.psum(partial_value, "bl")
    share_width = width // lax.axis_size("bl")
    result = lax.dynamic_slice_in_dim(totals, lax.axis_index("bl") * share_width, share_width, 2)
    return result


def solution(mesh):
    return jax.shard_map(
        per_device,
        mesh=mesh,
        in_specs=(P(None, "bl", "ma"), P("ma", None, "bl", None), P("bl", None), P(), P()),
        out_specs=P(None, "ma", "bl"),
        check_vma=False,
    )
```

profile of v0, /device:TPU:8, one launch (start us, length us, event | category | flops | bytes accessed | tf_op | source)
XLA Modules:
  0.0 123.3 jit_solution(16303524143769065953)
XLA Ops:
  0.0 0.0 copy-start
  0.0 14.5 %copy.16 = bf16[2,2080,256]{2,0,1:T(2,128)(2,1)} copy(bf16[2,2080,256]{2,1,0:T(8,128)(2,1)} %param.5) | data formatting | bytes 4259840 | tf_op args[0]
  14.5 0.0 copy-start.2
  14.5 0.0 copy-start.3
  14.5 9.9 %all-to-all-start = ((bf16[2,2080,256]{2,0,1:T(2,128)(2,1)}), bf16[2,2080,256]{2,0,1:T(2,128)(2,1)S(1)}, u32[]{:S(2)}, u32[]{:S(2)}) async-start(bf16[2,2080,256]{2,0,1:T(2,128)(2,1)} %copy.16), calls=%async_computation | async-start | bytes 4259840 | tf_op jit(solution)/shard_map/all_to_all | solution.py:29
  24.4 0.0 copy-done.2
  24.5 0.1 pad_add_fusion
  24.5 0.0 copy-done.3
  24.6 4.2 %fusion.24 = bf16[8192,32]{0,1:T(8,128)(2,1)S(1)} fusion(s32[32]{0:T(128)S(1)} %broadcast_add_fusion), kind=kLoop, calls=%fused_computation.29 | loop fusion | flops 4980736 | bytes 524416 | tf_op jit(solution)/shard_map/neg | solution.py:15
  28.8 5.2 %multiply_convert_fusion = (bf16[8192,32]{0,1:T(8,128)(2,1)S(1)}, bf16[8192,32]{0,1:T(8,128)(2,1)}) fusion(s32[32]{0:T(128)S(1)} %broadcast_add_fusion), kind=kLoop, calls=%fused_computation.24 | loop fusion | flops 4718592 | bytes 1048704 | tf_op jit(solution)/shard_map/convert_element_type | solution.py:14
  34.0 41.4 %all-to-all-done = bf16[2,2080,256]{2,0,1:T(2,128)(2,1)S(1)} async-done(((bf16[2,2080,256]{2,0,1:T(2,128)(2,1)}), bf16[2,2080,256]{2,0,1:T(2,128)(2,1)S(1)}, u32[]{:S(2)}, u32[]{:S(2)}) %all-to-all-start) | async-done | bytes 2129952 | tf_op jit(solution)/shard_map/all_to_all | solution.py:29
  75.4 3.0 %fusion.31 = (bf16[1,65,32,256]{3,0,1,2:T(2,128)(2,1)S(1)}, bf16[1,65,32,256]{3,0,1,2:T(2,128)(2,1)S(1)}) fusion(bf16[2,65,32,256]{3,0,1,2:T(2,128)(2,1)S(1)} %bitcast.38), kind=kLoop, calls=%fused_computation.53 | loop fusion | bytes 4259840 | tf_op jit(solution)/shard_map/slice | solution.py:21
  78.4 0.6 copy_bitcast_fusion
  79.0 0.1 pad.16
  79.1 0.7 copy.22
  79.9 0.0 copy-start.1
  79.9 0.1 pad.17
  80.0 0.7 copy.23
  80.7 0.2 copy-done.1
  80.9 0.9 fusion.13
  81.9 0.6 copy.19
  82.5 4.8 %all-to-all-start.1 = ((bf16[2,65,32]{1,0,2:T(2,128)(2,1)}), bf16[2,65,32]{1,0,2:T(2,128)(2,1)S(1)}, u32[]{:S(2)}, u32[]{:S(2)}) async-start(bf16[2,65,32]{1,0,2:T(2,128)(2,1)} %copy.19), calls=%async_computation.1 | async-start | bytes 32768 | tf_op jit(solution)/shard_map/all_to_all | solution.py:33
  87.3 0.0 copy-done
  87.3 7.6 %fusion = f32[4160,2]{0,1:T(2,128)S(1)} fusion(f32[2,1024]{1,0:T(2,128)S(1)} %copy-done, s32[4160]{0:T(1024)S(1)} %pad_add_fusion), kind=kOutput, calls=%fused_computation.1 | convolution fusion | flops 106496000 | bytes 58112 | tf_op jit(solution)/shard_map/dot_general | solution.py:39
  94.9 0.3 all-to-all-done.1
  95.2 0.1 fusion.28
  95.3 0.1 reshape.63
  95.4 0.1 reshape.64
  95.5 0.1 add_convert_fusion
  95.6 0.1 maximum_bitcast_fusion
  95.7 0.1 pad_maximum_fusion
  95.8 4.6 %convolution_bitcast_fusion = f32[2,1,1000]{2,0,1:T(2,128)S(1)} fusion(bf16[4160,1000]{1,0:T(8,128)(2,1)} %bitcast.37, bf16[2,4160,1]{1,2,0:T(2,128)(2,1)S(1)} %pad_maximum_fusion), kind=kOutput, calls=%fused_computation.18 | convolution fusion | flops 16640000 | bytes 8344640 | tf_op jit(solution)/shard_map/mkc,mcl->kml/dot_general | solution.py:62
  100.4 22.2 %psum.7 = f32[2,1,1000]{2,0,1:T(2,128)S(1)} all-reduce(f32[2,1,1000]{2,0,1:T(2,128)S(1)} %convolution_bitcast_fusion), channel_id=1, replica_groups=mesh['ma'=32,'bl'=8] {'bl'}, use_global_device_ids=true, to_apply=%region_0.1 | all-reduce | flops 2000 | bytes 16000 | tf_op jit(solution)/shard_map/psum | solution.py:65
  122.7 0.6 constant_dynamic-slice_fusion
  (5 shorter events, 0.1 us)
Async XLA Ops:
  0.0 87.3 %copy-start = (f32[2,1024]{1,0:T(2,128)S(1)}, f32[2,1024]{1,0:T(2,128)}, u32[]{:S(2)}) copy-start(f32[2,1024]{1,0:T(2,128)} %param.8) | copy-start | bytes 24580
  14.5 9.9 %copy-start.2 = (s32[2080,2]{0,1:T(2,128)S(1)}, s32[2080,2]{0,1:T(2,128)}, u32[]{:S(2)}) copy-start(s32[2080,2]{0,1:T(2,128)} %param.7) | copy-start | bytes 49924
  14.5 10.1 %copy-start.3 = (s32[32]{0:T(128)S(1)}, s32[32]{0:T(128)}, u32[]{:S(2)}) copy-start(s32[32]{0:T(128)} %param.9) | copy-start | bytes 388
  14.5 60.9 %all-to-all-start = ((bf16[2,2080,256]{2,0,1:T(2,128)(2,1)}), bf16[2,2080,256]{2,0,1:T(2,128)(2,1)S(1)}, u32[]{:S(2)}, u32[]{:S(2)}) async-start(bf16[2,2080,256]{2,0,1:T(2,128)(2,1)} %copy.16), calls=%async_computation | async-start | bytes 4259840 | tf_op jit(solution)/shard_map/all_to_all | solution.py:29
  79.9 1.0 copy-start.1
  82.5 12.7 %all-to-all-start.1 = ((bf16[2,65,32]{1,0,2:T(2,128)(2,1)}), bf16[2,65,32]{1,0,2:T(2,128)(2,1)S(1)}, u32[]{:S(2)}, u32[]{:S(2)}) async-start(bf16[2,65,32]{1,0,2:T(2,128)(2,1)} %copy.19), calls=%async_computation.1 | async-start | bytes 32768 | tf_op jit(solution)/shard_map/all_to_all | solution.py:33
where the time goes:
time: 125 us; the launch traced here: 123 us
  waiting for transfers between devices  41.7 us (33%)
  blocking collectives  22.2 us (18%)
  local copies, waits for them, and re-layouts  21.5 us (17%)
  starting transfers between devices  14.7 us (12%)
  matrix products  13.1 us (10%)
  other arithmetic  9.92 us (8%)
    all_to_all x1, waiting for transfers between devices, per_device(): lax.all_to_all(visibilities, 'ma', split_axis=1, concat_axis=2, tiled=True)  41.4 us
    psum x1, blocking collectives, per_device(): totals = lax.psum(partial_value, 'bl')  22.2 us
    unnamed x14, local copies, waits for them, and re-layouts  16.9 us
    all_to_all x1, starting transfers between devices, per_device(): lax.all_to_all(visibilities, 'ma', split_axis=1, concat_axis=2, tiled=True)  9.91 us
    dot_general x1, matrix products, per_device(): jnp.dot(one_hot, jnp.transpose(feed_gains), precision=lax.Precision.HIGHE...  7.6 us
    convert_element_type x1, other arithmetic, dft_weights(): sin_part = (jnp.sin(phases) * scale).astype(jnp.bfloat16)  5.22 us
    all_to_all x1, starting transfers between devices, per_device(): lax.all_to_all(spectra_all, 'ma', split_axis=2, concat_axis=1, tiled=True)  4.8 us
    dot_general x1, matrix products, per_device(): jnp.einsum('mkc,mcl->kml', vectors, flat_blocks, preferred_element_type=j...  4.63 us
  transfers between devices with their start and end apart: 2, of which 2 were waited for; matrix products, arithmetic and copies ran while one was open for 14% of the time, Pallas kernels for 0%

commit v1 on v0

v1 whole, which is shorter than its diff:
```python
import jax
import jax.numpy as jnp
from jax import lax
from jax.experimental import pallas as pl
from jax.experimental.pallas import tpu as pltpu
from jax.sharding import PartitionSpec as P

NT = 8192
GROUPS = 4
LANES = 128


def group_spans(rows):
    step = rows // GROUPS // LANES * LANES
    starts = [group * step for group in range(GROUPS)]
    return [(start, (starts[i + 1] if i + 1 < GROUPS else rows) - start) for i, start in enumerate(starts)]


def lane_pieces(size):
    return [(at, min(LANES, size - at)) for at in range(0, size, LANES)]


def padded(size):
    return -(-size // LANES) * LANES


def transform_kernel(spans, first_time, m_ref, vis_ref, out_ref, held, lines, sems):
    copies = []
    for group, (start, size) in enumerate(spans):
        rows = pl.ds(start, size)
        copy = pltpu.make_async_copy(vis_ref.at[:, rows, :], held.at[:, rows, :], sems.at[group])
        copy.start()
        copies.append(copy)
    count = m_ref.shape[0]
    times = vis_ref.shape[2]
    slot = lax.broadcasted_iota(jnp.int32, (count, LANES), 0)
    m_values = jnp.zeros((count, LANES), jnp.int32)
    for j in range(count):
        m_values = jnp.where(slot == j, m_ref[j] - count // 2, m_values)
    begin = first_time() * times
    scale = 1.0 / jnp.sqrt(jnp.float32(NT))
    cos_parts, sin_parts = [], []
    for at in range(0, times, LANES):
        t = begin + at + lax.broadcasted_iota(jnp.int32, (count, LANES), 1)
        wrapped = jnp.bitwise_and(t * m_values, NT - 1).astype(jnp.float32)
        phases = wrapped * (2.0 * jnp.pi / NT)
        cos_parts.append(jnp.cos(phases) * scale)
        sin_parts.append(jnp.sin(phases) * scale)
    cos_part = jnp.concatenate(cos_parts, axis=1)
    sin_part = jnp.concatenate(sin_parts, axis=1)
    for_real = jnp.concatenate([cos_part, -sin_part], axis=0).astype(jnp.bfloat16)
    for_imag = jnp.concatenate([sin_part, cos_part], axis=0).astype(jnp.bfloat16)
    lines[...] = jnp.zeros_like(lines)
    contract = (((1,), (1,)), ((), ()))
    for group, (start, size) in enumerate(spans):
        copies[group].wait()
        rows = pl.ds(start, size)
        found = lax.dot_general(for_real, held[0, rows, :], contract, preferred_element_type=jnp.float32)
        found += lax.dot_general(for_imag, held[1, rows, :], contract, preferred_element_type=jnp.float32)
        for piece, (at, width) in enumerate(lane_pieces(size)):
            for part in range(2):
                lines[piece, pl.ds(part * GROUPS + group, count, stride=2 * GROUPS), :width] = found[
                    part * count:(part + 1) * count, at:at + width
                ]
    for piece in range(lines.shape[0]):
        block = lines[piece].reshape(count, 2 * GROUPS, LANES)
        out_ref[:, :, piece * LANES:(piece + 1) * LANES] = block.astype(jnp.bfloat16)


def transform(visibilities, m_order, axis):
    rows, times = visibilities.shape[1:]
    count = m_order.shape[0]
    spans = group_spans(rows)
    width = padded(max(size for _, size in spans))

    def body(begin_ref, *refs):
        transform_kernel(spans, lambda: begin_ref[0], *refs)

    return pl.pallas_call(
        body,
        out_shape=jax.ShapeDtypeStruct((count, 2 * GROUPS, width), jnp.bfloat16),
        in_specs=[
            pl.BlockSpec(memory_space=pltpu.SMEM),
            pl.BlockSpec(memory_space=pltpu.SMEM),
            pl.BlockSpec(memory_space=pl.ANY),
        ],
        out_specs=pl.BlockSpec(memory_space=pltpu.VMEM),
        scratch_shapes=[
            pltpu.VMEM((2, rows, times), jnp.bfloat16),
            pltpu.VMEM((width // LANES, count * 2 * GROUPS, LANES), jnp.float32),
            pltpu.SemaphoreType.DMA((GROUPS,)),
        ],
        name="transform",
    )(lax.axis_index(axis).reshape(1), m_order, visibilities)


def three_pieces(value):
    first = value.astype(jnp.bfloat16)
    rest = value - first.astype(jnp.float32)
    second = rest.astype(jnp.bfloat16)
    third = (rest - second.astype(jnp.float32)).astype(jnp.bfloat16)
    return [first, second, third]


def factor_kernel(spans, pairs_ref, gains_ref, out_ref):
    feeds = gains_ref.shape[1]
    tiles = feeds // LANES
    table = jnp.concatenate(
        [gains_ref[part:part + 1, tile * LANES:(tile + 1) * LANES] for part in range(2) for tile in range(tiles)], axis=0
    )
    pieces = jnp.concatenate(three_pieces(table), axis=0)
    tall = 2 * tiles
    out_ref[...] = jnp.zeros_like(out_ref)
    for group, (start, size) in enumerate(spans):
        picked = []
        for side in range(2):
            feed = pairs_ref[side:side + 1, pl.ds(start, size)]
            lane = jnp.bitwise_and(feed, LANES - 1)
            tile = lax.shift_right_logical(feed, LANES.bit_length() - 1)
            lane_iota = lax.broadcasted_iota(jnp.int32, (LANES, size), 0)
            one_hot = jnp.where(lane_iota == lane, 1.0, 0.0).astype(jnp.bfloat16)
            rows = jnp.dot(pieces, one_hot, preferred_element_type=jnp.float32)
            whole = (rows[:tall] + rows[tall:2 * tall]) + rows[2 * tall:]
            chosen = lax.broadcasted_iota(jnp.int32, (tiles, size), 0) == tile
            for part in range(2):
                picked.append(jnp.sum(jnp.where(chosen, whole[part * tiles:(part + 1) * tiles], 0.0), axis=0, keepdims=True))
        a_re, a_im, b_re, b_im = picked
        factor_re = a_re * b_re + a_im * b_im
        factor_im = a_im * b_re - a_re * b_im
        out_ref[0, group:group + 1, :size] = factor_re
        out_ref[0, GROUPS + group:GROUPS + group + 1, :size] = factor_re
        out_ref[1, group:group + 1, :size] = -factor_im
        out_ref[1, GROUPS + group:GROUPS + group + 1, :size] = factor_im


def factors(feed_pairs, feed_gains):
    rows = feed_pairs.shape[0]
    spans = group_spans(rows)
    width = padded(max(size for _, size in spans))

    def body(*refs):
        factor_kernel(spans, *refs)

    return pl.pallas_call(
        body,
        out_shape=jax.ShapeDtypeStruct((2, 2 * GROUPS, width), jnp.float32),
        in_specs=[pl.BlockSpec(memory_space=pltpu.VMEM)] * 2,
        out_specs=pl.BlockSpec(memory_space=pltpu.VMEM),
        cost_estimate=pl.CostEstimate(flops=2 * 2 * rows * 48 * 128, bytes_accessed=rows * 8 + 8192 + 40960, transcendentals=0),
        name="factors",
    )(jnp.transpose(feed_pairs), feed_gains)


def project_kernel(spans, shares, got_ref, factor_ref, beam_ref, out_ref, held, sems):
    copies = []
    for part in range(2):
        for group, (start, size) in enumerate(spans):
            rows = pl.ds(start, size)
            copy = pltpu.make_async_copy(
                beam_ref.at[0, part, rows, :], held.at[part, rows, :], sems.at[part * GROUPS + group]
            )
            copy.start()
            copies.append(copy)
    total = got_ref[0].astype(jnp.float32)
    for source in range(1, got_ref.shape[0]):
        total += got_ref[source].astype(jnp.float32)
    swapped = jnp.concatenate([total[GROUPS:], total[:GROUPS]], axis=0)
    weighted = total * factor_ref[0] + swapped * factor_ref[1]
    high = weighted.astype(jnp.bfloat16)
    low = (weighted - high.astype(jnp.float32)).astype(jnp.bfloat16)
    rows16 = jnp.concatenate([high.astype(jnp.float32), low.astype(jnp.float32)], axis=0)
    row_group = jnp.bitwise_and(lax.broadcasted_iota(jnp.int32, rows16.shape, 0), GROUPS - 1)
    lefts = [jnp.where(row_group == group, rows16, 0.0).astype(jnp.bfloat16) for group in range(GROUPS)]
    sums = []
    for part in range(2):
        value = None
        for group, (start, size) in enumerate(spans):
            copies[part * GROUPS + group].wait()
            term = jnp.dot(lefts[group][:, :size], held[part, pl.ds(start, size), :], preferred_element_type=jnp.float32)
            value = term if value is None else value + term
        value = value[:2 * GROUPS] + value[2 * GROUPS:]
        sums.append(
            [jnp.sum(value[piece * GROUPS:(piece + 1) * GROUPS], axis=0, keepdims=True) for piece in range(2)]
        )
    answer = jnp.concatenate([sums[0][0] + sums[1][1], sums[0][1] - sums[1][0]], axis=0)
    width = answer.shape[1]
    share = width // shares
    for k in range(shares):
        out_ref[k, :, :share] = answer[:, k * share:(k + 1) * share]


def project(got, factor, beam_blocks, shares):
    rows, width = beam_blocks.shape[2:]
    spans = group_spans(rows)

    def body(*refs):
        project_kernel(spans, shares, *refs)

    return pl.pallas_call(
        body,
        out_shape=jax.ShapeDtypeStruct((shares, 2, padded(width // shares)), jnp.float32),
        in_specs=[
            pl.BlockSpec(memory_space=pltpu.VMEM),
            pl.BlockSpec(memory_space=pltpu.VMEM),
            pl.BlockSpec(memory_space=pl.ANY),
        ],
        out_specs=pl.BlockSpec(memory_space=pltpu.VMEM),
        scratch_shapes=[
            pltpu.VMEM((2, rows, width), jnp.bfloat16),
            pltpu.SemaphoreType.DMA((2 * GROUPS,)),
        ],
        compiler_params=pltpu.CompilerParams(vmem_limit_bytes=32 * 1024 * 1024),
        name="project",
    )(got, factor, beam_blocks)


def per_device(visibilities, beam_blocks, feed_pairs, feed_gains, m_order):
    shares = lax.axis_size("bl")
    share_width = beam_blocks.shape[3] // shares
    partial_spectra = transform(visibilities, m_order, "ma")
    got = lax.all_to_all(partial_spectra, "ma", split_axis=0, concat_axis=0, tiled=True)
    factor = factors(feed_pairs, feed_gains)
    partial_modes = project(got, factor, beam_blocks, shares)
    parts = lax.all_to_all(partial_modes, "bl", split_axis=0, concat_axis=0, tiled=True)
    return jnp.sum(parts, axis=0)[:, None, :share_width]


def solution(mesh):
    return jax.shard_map(
        per_device,
        mesh=mesh,
        in_specs=(P(None, "bl", "ma"), P("ma", None, "bl", None), P("bl", None), P(), P()),
        out_specs=P(None, "ma", "bl"),
        check_vma=False,
    )
```

time: 125 us -> 48.4 us (0.39)
  waiting for transfers between devices: 41.7 us -> 12.2 us
  local copies, waits for them, and re-layouts: 21.5 us -> 4.2 us
  matrix products: 13.1 us -> 0 us
  other arithmetic: 9.92 us -> 0.58 us
  blocking collectives: 22.2 us -> 13.1 us
  Pallas kernels: 0 us -> 7.79 us
  starting transfers between devices: 14.7 us -> 9.79 us
    all_to_all x2 -> x1, waiting for transfers between devices: 41.7 us -> 12.2 us  [per_device(): lax.all_to_all(partial_spectra, 'ma', split_axis=0, concat_axis=0, tiled=...]
    psum x1 -> x0, blocking collectives: 22.2 us -> none  [per_device(): totals = lax.psum(partial_value, 'bl')]
    dot_general x3 -> x0, matrix products: 13.1 us -> none  [the longest x1 7.6 us: per_device(): jnp.dot(one_hot, jnp.transpose(feed_gains), precision=lax.Precision.HIGHE...]
    all_to_all x0 -> x1, blocking collectives: none -> 13.1 us  [per_device(): lax.all_to_all(partial_modes, 'bl', split_axis=0, concat_axis=0, tiled=True)]
    unnamed x14 -> x4, local copies, waits for them, and re-layouts: 16.9 us -> 4.2 us
    pallas_call x0 -> x3, Pallas kernels: none -> 7.79 us  [the longest x1 3.68 us: transform(): pl.pallas_call(body, out_shape=jax.ShapeDtypeStruct((count, 2 * GROUPS, w...]
    convert_element_type x3 -> x0, other arithmetic: 5.42 us -> none  [the longest x1 5.22 us: dft_weights(): sin_part = (jnp.sin(phases) * scale).astype(jnp.bfloat16)]
    all_to_all x2 -> x1, starting transfers between devices: 14.7 us -> 9.79 us  [per_device(): lax.all_to_all(partial_spectra, 'ma', split_axis=0, concat_axis=0, tiled=...]
  transfers between devices with their start and end apart: 2 -> 1, of which waited for: 2 -> 1; matrix products, arithmetic and copies ran while one was open for 14% -> 0% of each run, Pallas kernels for 0% -> 3%
where the time goes in v1:
time: 48.4 us; the launch traced here: 47.7 us
  blocking collectives  13.1 us (27%)
  waiting for transfers between devices  12.2 us (25%)
  starting transfers between devices  9.79 us (20%)
  Pallas kernels  7.79 us (16%)
  local copies, waits for them, and re-layouts  4.2 us (9%)
  other arithmetic  0.58 us (1%)
    all_to_all x1, blocking collectives, per_device(): lax.all_to_all(partial_modes, 'bl', split_axis=0, concat_axis=0, tiled=True)  13.1 us
    all_to_all x1, waiting for transfers between devices, per_device(): lax.all_to_all(partial_spectra, 'ma', split_axis=0, concat_axis=0, tiled=...  12.2 us
    all_to_all x1, starting transfers between devices, per_device(): lax.all_to_all(partial_spectra, 'ma', split_axis=0, concat_axis=0, tiled=...  9.79 us
    unnamed x4, local copies, waits for them, and re-layouts  4.2 us
    pallas_call x1, Pallas kernels, transform(): pl.pallas_call(body, out_shape=jax.ShapeDtypeStruct((count, 2 * GROUPS, w...  3.68 us
    pallas_call x1, Pallas kernels, project(): pl.pallas_call(body, out_shape=jax.ShapeDtypeStruct((shares, 2, padded(wi...  2.46 us
    pallas_call x1, Pallas kernels, factors(): pl.pallas_call(body, out_shape=jax.ShapeDtypeStruct((2, 2 * GROUPS, width...  1.65 us
  transfers between devices with their start and end apart: 1, of which 1 were waited for; matrix products, arithmetic and copies ran while one was open for 0% of the time, Pallas kernels for 3%

profile of v1, /device:TPU:8, one launch (start us, length us, event | category | flops | bytes accessed | tf_op | source)
XLA Modules:
  0.0 47.7 jit_solution(14247385264418599426)
XLA Ops:
  0.0 3.7 %transform.1 = bf16[32,8,640]{2,1,0:T(8,128)(2,1)} custom-call(s32[1]{0:T(128)} %bitcast.begin_ref, s32[32]{0:T(128)} %refs_0_.1, bf16[2,2080,256]{2,1,0:T(8,128)(2,1)} %refs_1_.2), custom_call_target="tpu_custom_call" | custom-call | tf_op jit(solution)/shard_map/transform/pallas_call | solution.py:79
  3.7 9.8 %all-to-all-start = ((bf16[32,8,640]{2,1,0:T(8,128)(2,1)}), bf16[32,8,640]{2,1,0:T(8,128)(2,1)S(1)}, u32[]{:S(2)}, u32[]{:S(2)}) async-start(bf16[32,8,640]{2,1,0:T(8,128)(2,1)} %transform.1), calls=%async_computation | async-start | bytes 655360 | tf_op jit(solution)/shard_map/all_to_all | solution.py:221
  13.5 1.7 %factors.1.refs_1_ = f32[2,8,640]{2,1,0:T(8,128)} custom-call(s32[2,2080]{1,0:T(2,128)} %bitcast.5, f32[2,1024]{1,0:T(2,128)} %refs_1_.3), custom_call_target="tpu_custom_call" | custom-call | flops 51118080 | bytes 65792 | tf_op jit(solution)/shard_map/factors/pallas_call | solution.py:144
  15.1 12.2 %all-to-all-done.refs_0_ = bf16[32,8,640]{2,1,0:T(8,128)(2,1)S(1)} async-done(((bf16[32,8,640]{2,1,0:T(8,128)(2,1)}), bf16[32,8,640]{2,1,0:T(8,128)(2,1)S(1)}, u32[]{:S(2)}, u32[]{:S(2)}) %all-to-all-start) | async-done | bytes 327712 | tf_op jit(solution)/shard_map/all_to_all | solution.py:221
  27.3 0.0 copy-start
  27.3 3.4 %copy-done = bf16[1,2,2080,1000]{3,2,1,0:T(8,128)(2,1)S(1)} copy-done((bf16[1,2,2080,1000]{3,2,1,0:T(8,128)(2,1)S(1)}, bf16[1,2,2080,1000]{3,2,1,0:T(8,128)(2,1)}, u32[]{:S(2)}) %copy-start) | copy-done | bytes 8320024
  30.7 0.0 copy-start.1
  30.7 0.8 %copy-done.1 = f32[2,8,640]{2,1,0:T(8,128)S(1)} copy-done((f32[2,8,640]{2,1,0:T(8,128)S(1)}, f32[2,8,640]{2,1,0:T(8,128)}, u32[]{:S(2)}) %copy-start.1) | copy-done | bytes 40984
  31.5 2.5 %project.1 = f32[8,2,128]{2,1,0:T(2,128)S(1)} custom-call(bf16[32,8,640]{2,1,0:T(8,128)(2,1)S(1)} %all-to-all-done.refs_0_, f32[2,8,640]{2,1,0:T(8,128)S(1)} %copy-done.1, bf16[1,2,2080,1000]{3,2,1,0:T(8,128)(2,1)S(1)} %copy-done), custom_call_target="tpu_custom_call" | custom-call | tf_op jit(solution)/shard_map/project/pallas_call | solution.py:199
  34.0 13.1 %all_to_all.10 = f32[8,2,128]{2,1,0:T(2,128)S(1)} all-to-all(f32[8,2,128]{2,1,0:T(2,128)S(1)} %project.1), channel_id=1, replica_groups=mesh['ma'=32,'bl'=8] {'bl'}, dimensions={0} | all-to-all | bytes 16384 | tf_op jit(solution)/shard_map/all_to_all | solution.py:224
  47.1 0.6 %reduce_sum.9 = f32[2,128]{1,0:T(2,128)} reduce(f32[8,2,128]{2,1,0:T(2,128)S(1)} %all_to_all.10, f32[]{:T(128)} %constant.7.clone.1), dimensions={0}, to_apply=%region_0.0 | reduce | flops 1792 | bytes 9220 | tf_op jit(solution)/shard_map/reduce_sum | solution.py:225
Async XLA Ops:
  3.7 23.6 %all-to-all-start = ((bf16[32,8,640]{2,1,0:T(8,128)(2,1)}), bf16[32,8,640]{2,1,0:T(8,128)(2,1)S(1)}, u32[]{:S(2)}, u32[]{:S(2)}) async-start(bf16[32,8,640]{2,1,0:T(8,128)(2,1)} %transform.1), calls=%async_computation | async-start | bytes 655360 | tf_op jit(solution)/shard_map/all_to_all | solution.py:221
  27.3 3.4 %copy-start = (bf16[1,2,2080,1000]{3,2,1,0:T(8,128)(2,1)S(1)}, bf16[1,2,2080,1000]{3,2,1,0:T(8,128)(2,1)}, u32[]{:S(2)}) copy-start(bf16[1,2,2080,1000]{3,2,1,0:T(8,128)(2,1)} %refs_2_.1) | copy-start | bytes 24960004
  30.7 0.8 %copy-start.1 = (f32[2,8,640]{2,1,0:T(8,128)S(1)}, f32[2,8,640]{2,1,0:T(8,128)}, u32[]{:S(2)}) copy-start(f32[2,8,640]{2,1,0:T(8,128)} %factors.1.refs_1_) | copy-start | bytes 122884

commit v2 on v1

--- a/solution.py
+++ b/solution.py
@@ -7,7 +7,9 @@
 
 NT = 8192
 GROUPS = 4
+EARLY = 3
 LANES = 128
+MIB = 1024 * 1024
 
 
 def group_spans(rows):
@@ -24,7 +26,7 @@
     return -(-size // LANES) * LANES
 
 
-def transform_kernel(spans, first_time, m_ref, vis_ref, out_ref, held, lines, sems):
+def transform_kernel(spans, my_slot, m_ref, vis_ref, keep_ref, send_ref, held, lines, sems):
     copies = []
     for group, (start, size) in enumerate(spans):
         rows = pl.ds(start, size)
@@ -32,12 +34,15 @@
         copy.start()
         copies.append(copy)
     count = m_ref.shape[0]
+    half = count // 2
     times = vis_ref.shape[2]
-    slot = lax.broadcasted_iota(jnp.int32, (count, LANES), 0)
+    parity = jnp.bitwise_and(my_slot, 1)
+    row = lax.broadcasted_iota(jnp.int32, (count, LANES), 0)
     m_values = jnp.zeros((count, LANES), jnp.int32)
-    for j in range(count):
-        m_values = jnp.where(slot == j, m_ref[j] - count // 2, m_values)
-    begin = first_time() * times
+    for i in range(half):
+        m_values = jnp.where(row == i, m_ref[2 * i + parity] - count // 2, m_values)
+        m_values = jnp.where(row == half + i, m_ref[2 * i + 1 - parity] - count // 2, m_values)
+    begin = my_slot * times
     scale = 1.0 / jnp.sqrt(jnp.float32(NT))
     cos_parts, sin_parts = [], []
     for at in range(0, times, LANES):
@@ -50,48 +55,51 @@
     sin_part = jnp.concatenate(sin_parts, axis=1)
     for_real = jnp.concatenate([cos_part, -sin_part], axis=0).astype(jnp.bfloat16)
     for_imag = jnp.concatenate([sin_part, cos_part], axis=0).astype(jnp.bfloat16)
-    lines[...] = jnp.zeros_like(lines)
     contract = (((1,), (1,)), ((), ()))
     for group, (start, size) in enumerate(spans):
         copies[group].wait()
         rows = pl.ds(start, size)
         found = lax.dot_general(for_real, held[0, rows, :], contract, preferred_element_type=jnp.float32)
         found += lax.dot_general(for_imag, held[1, rows, :], contract, preferred_element_type=jnp.float32)
-        for piece, (at, width) in enumerate(lane_pieces(size)):
+        for piece, (at, width) in enumerate(lane_pieces(lines.shape[0] * LANES)):
             for part in range(2):
-                lines[piece, pl.ds(part * GROUPS + group, count, stride=2 * GROUPS), :width] = found[
-                    part * count:(part + 1) * count, at:at + width
-                ]
+                to = pl.ds(part * GROUPS + group, count, stride=2 * GROUPS)
+                filled = min(width, max(size - at, 0))
+                if filled < width:
+                    lines[piece, to, :] = jnp.zeros((count, width), jnp.float32)
+                if filled > 0:
+                    lines[piece, to, :filled] = found[part * count:(part + 1) * count, at:at + filled]
     for piece in range(lines.shape[0]):
         block = lines[piece].reshape(count, 2 * GROUPS, LANES)
-        out_ref[:, :, piece * LANES:(piece + 1) * LANES] = block.astype(jnp.bfloat16)
-
-
-def transform(visibilities, m_order, axis):
+        keep_ref[:, :, piece * LANES:(piece + 1) * LANES] = block[:half]
+        send_ref[:, :, piece * LANES:(piece + 1) * LANES] = block[half:]
+
+
+def transform(visibilities, m_order, slot):
     rows, times = visibilities.shape[1:]
     count = m_order.shape[0]
     spans = group_spans(rows)
     width = padded(max(size for _, size in spans))
 
-    def body(begin_ref, *refs):
-        transform_kernel(spans, lambda: begin_ref[0], *refs)
+    def body(slot_ref, *refs):
+        transform_kernel(spans, slot_ref[0], *refs)
 
     return pl.pallas_call(
         body,
-        out_shape=jax.ShapeDtypeStruct((count, 2 * GROUPS, width), jnp.bfloat16),
+        out_shape=[jax.ShapeDtypeStruct((count // 2, 2 * GROUPS, width), jnp.float32)] * 2,
         in_specs=[
             pl.BlockSpec(memory_space=pltpu.SMEM),
             pl.BlockSpec(memory_space=pltpu.SMEM),
             pl.BlockSpec(memory_space=pl.ANY),
         ],
-        out_specs=pl.BlockSpec(memory_space=pltpu.VMEM),
+        out_specs=[pl.BlockSpec(memory_space=pltpu.VMEM)] * 2,
         scratch_shapes=[
             pltpu.VMEM((2, rows, times), jnp.bfloat16),
             pltpu.VMEM((width // LANES, count * 2 * GROUPS, LANES), jnp.float32),
             pltpu.SemaphoreType.DMA((GROUPS,)),
         ],
         name="transform",
-    )(lax.axis_index(axis).reshape(1), m_order, visibilities)
+    )(slot.reshape(1), m_order, pltpu.with_memory_space_constraint(visibilities, pltpu.HBM))
 
 
 def three_pieces(value):
@@ -102,7 +110,9 @@
     return [first, second, third]
 
 
-def factor_kernel(spans, pairs_ref, gains_ref, out_ref):
+def factor_kernel(spans, pairs_ref, gains_ref, beam_ref, out_ref, held_ref, sem):
+    copy = pltpu.make_async_copy(beam_ref.at[0, 0, pl.ds(0, held_ref.shape[0]), :], held_ref, sem)
+    copy.start()
     feeds = gains_ref.shape[1]
     tiles = feeds // LANES
     table = jnp.concatenate(
@@ -131,36 +141,51 @@
         out_ref[0, GROUPS + group:GROUPS + group + 1, :size] = factor_re
         out_ref[1, group:group + 1, :size] = -factor_im
         out_ref[1, GROUPS + group:GROUPS + group + 1, :size] = factor_im
-
-
-def factors(feed_pairs, feed_gains):
-    rows = feed_pairs.shape[0]
+    copy.wait()
+
+
+def factors(feed_pairs, feed_gains, beam_blocks):
+    rows, width = beam_blocks.shape[2:]
     spans = group_spans(rows)
-    width = padded(max(size for _, size in spans))
+    line = padded(max(size for _, size in spans))
 
     def body(*refs):
         factor_kernel(spans, *refs)
 
     return pl.pallas_call(
         body,
-        out_shape=jax.ShapeDtypeStruct((2, 2 * GROUPS, width), jnp.float32),
-        in_specs=[pl.BlockSpec(memory_space=pltpu.VMEM)] * 2,
-        out_specs=pl.BlockSpec(memory_space=pltpu.VMEM),
-        cost_estimate=pl.CostEstimate(flops=2 * 2 * rows * 48 * 128, bytes_accessed=rows * 8 + 8192 + 40960, transcendentals=0),
+        out_shape=[
+            pltpu.VMEM((2, 2 * GROUPS, line), jnp.float32),
+            pltpu.VMEM((spans[EARLY][0], width), jnp.bfloat16),
+        ],
+        in_specs=[
+            pl.BlockSpec(memory_space=pltpu.VMEM),
+            pl.BlockSpec(memory_space=pltpu.VMEM),
+            pl.BlockSpec(memory_space=pltpu.HBM),
+        ],
+        out_specs=[pl.BlockSpec(memory_space=pltpu.VMEM)] * 2,
+        scratch_shapes=[pltpu.SemaphoreType.DMA],
+        cost_estimate=pl.CostEstimate(
+            flops=2 * 2 * rows * 48 * 128, bytes_accessed=2 * spans[EARLY][0] * width + 8 * rows, transcendentals=0
+        ),
+        compiler_params=pltpu.CompilerParams(vmem_limit_bytes=16 * MIB),
         name="factors",
-    )(jnp.transpose(feed_pairs), feed_gains)
-
-
-def project_kernel(spans, shares, got_ref, factor_ref, beam_ref, out_ref, held, sems):
-    copies = []
+    )(jnp.transpose(feed_pairs), feed_gains, pltpu.with_memory_space_constraint(beam_blocks, pltpu.HBM))
+
+
+def project_kernel(spans, shares, got_ref, factor_ref, early_ref, beam_ref, out_ref, held, sems):
+    copies = {}
     for part in range(2):
         for group, (start, size) in enumerate(spans):
+            if part == 0 and group < EARLY:
+                continue
             rows = pl.ds(start, size)
-            copy = pltpu.make_async_copy(
-                beam_ref.at[0, part, rows, :], held.at[part, rows, :], sems.at[part * GROUPS + group]
+            copies[part, group] = pltpu.make_async_copy(
+                beam_ref.at[0, part, rows, :],
+                held.at[pl.ds(part * spans[-1][1] + (start if part else 0), size), :],
+                sems.at[part * GROUPS + group],
             )
-            copy.start()
-            copies.append(copy)
+            copies[part, group].start()
     total = got_ref[0].astype(jnp.float32)
     for source in range(1, got_ref.shape[0]):
         total += got_ref[source].astype(jnp.float32)
@@ -175,8 +200,12 @@
     for part in range(2):
         value = None
         for group, (start, size) in enumerate(spans):
-            copies[part * GROUPS + group].wait()
-            term = jnp.dot(lefts[group][:, :size], held[part, pl.ds(start, size), :], preferred_element_type=jnp.float32)
+            if (part, group) in copies:
+                copies[part, group].wait()
+                right = held[pl.ds(part * spans[-1][1] + (start if part else 0), size), :]
+            else:
+                right = early_ref[pl.ds(start, size), :]
+            term = jnp.dot(lefts[group][:, :size], right, preferred_element_type=jnp.float32)
             value = term if value is None else value + term
         value = value[:2 * GROUPS] + value[2 * GROUPS:]
         sums.append(
@@ -189,7 +218,7 @@
         out_ref[k, :, :share] = answer[:, k * share:(k + 1) * share]
 
 
-def project(got, factor, beam_blocks, shares):
+def project(got, factor, early, beam_blocks, shares):
     rows, width = beam_blocks.shape[2:]
     spans = group_spans(rows)
 
@@ -199,28 +228,31 @@
     return pl.pallas_call(
         body,
         out_shape=jax.ShapeDtypeStruct((shares, 2, padded(width // shares)), jnp.float32),
-        in_specs=[
-            pl.BlockSpec(memory_space=pltpu.VMEM),
-            pl.BlockSpec(memory_space=pltpu.VMEM),
-            pl.BlockSpec(memory_space=pl.ANY),
-        ],
+        in_specs=[pl.BlockSpec(memory_space=pltpu.VMEM)] * 3 + [pl.BlockSpec(memory_space=pltpu.HBM)],
         out_specs=pl.BlockSpec(memory_space=pltpu.VMEM),
         scratch_shapes=[
-            pltpu.VMEM((2, rows, width), jnp.bfloat16),
+            pltpu.VMEM((spans[-1][1] + rows, width), jnp.bfloat16),
             pltpu.SemaphoreType.DMA((2 * GROUPS,)),
         ],
-        compiler_params=pltpu.CompilerParams(vmem_limit_bytes=32 * 1024 * 1024),
+        compiler_params=pltpu.CompilerParams(vmem_limit_bytes=24 * MIB),
         name="project",
-    )(got, factor, beam_blocks)
+    )(
+        *(pltpu.with_memory_space_constraint(held, pltpu.VMEM) for held in (got, factor, early)),
+        pltpu.with_memory_space_constraint(beam_blocks, pltpu.HBM),
+    )
 
 
 def per_device(visibilities, beam_blocks, feed_pairs, feed_gains, m_order):
     shares = lax.axis_size("bl")
+    slots = lax.axis_size("ma")
     share_width = beam_blocks.shape[3] // shares
-    partial_spectra = transform(visibilities, m_order, "ma")
-    got = lax.all_to_all(partial_spectra, "ma", split_axis=0, concat_axis=0, tiled=True)
-    factor = factors(feed_pairs, feed_gains)
-    partial_modes = project(got, factor, beam_blocks, shares)
+    keep, send = transform(visibilities, m_order, lax.axis_index("ma"))
+    other = lax.ppermute(send, "ma", [(slot, slot ^ 1) for slot in range(slots)])
+    pair = (keep + other).astype(jnp.bfloat16)
+    same_core = [[2 * i + parity for i in range(slots // 2)] for parity in range(2)]
+    got = lax.all_to_all(pair, "ma", split_axis=0, concat_axis=0, tiled=True, axis_index_groups=same_core)
+    factor, early = factors(feed_pairs, feed_gains, beam_blocks)
+    partial_modes = project(got, factor, early, beam_blocks, shares)
     parts = lax.all_to_all(partial_modes, "bl", split_axis=0, concat_axis=0, tiled=True)
     return jnp.sum(parts, axis=0)[:, None, :share_width]
 

time: 48.4 us -> 44.6 us (0.921)
  local copies, waits for them, and re-layouts: 4.2 us -> 0.01 us
  waiting for transfers between devices: 12.2 us -> 10.4 us
  other arithmetic: 0.58 us -> 2.27 us
  Pallas kernels: 7.79 us -> 8.81 us
    unnamed x4, local copies, waits for them, and re-layouts: 4.2 us -> 0.01 us
    all_to_all x1, waiting for transfers between devices: 12.2 us -> 8.61 us  [per_device(): lax.all_to_all(pair, 'ma', split_axis=0, concat_axis=0, tiled=True, axis_...]
    ppermute x0 -> x1, waiting for transfers between devices: none -> 1.83 us  [per_device(): lax.ppermute(send, 'ma', [(slot, slot ^ 1) for slot in range(slots)])]
    convert_element_type x0 -> x1, other arithmetic: none -> 1.69 us  [per_device(): pair = (keep + other).astype(jnp.bfloat16)]
    pallas_call x2, Pallas kernels: 5.33 us -> 5.85 us  [the longest x1 3.95 us: transform(): pl.pallas_call(body, out_shape=[jax.ShapeDtypeStruct((count // 2, 2 * GRO...]
    pallas_call x1, Pallas kernels: 2.46 us -> 2.96 us  [project(): pl.pallas_call(body, out_shape=jax.ShapeDtypeStruct((shares, 2, padded(wi...]
  transfers between devices with their start and end apart: 1 -> 2, of which waited for: 1 -> 2; matrix products, arithmetic and copies ran while one was open for 0% -> 0% of each run, Pallas kernels for 3% -> 4%
where the time goes in v2:
time: 44.6 us; the launch traced here: 44.3 us
  blocking collectives  13.1 us (29%)
  waiting for transfers between devices  10.4 us (23%)
  starting transfers between devices  9.59 us (22%)
  Pallas kernels  8.81 us (20%)
  other arithmetic  2.27 us (5%)
    all_to_all x1, blocking collectives, per_device(): lax.all_to_all(partial_modes, 'bl', split_axis=0, concat_axis=0, tiled=True)  13.1 us
    all_to_all x1, starting transfers between devices, per_device(): lax.all_to_all(pair, 'ma', split_axis=0, concat_axis=0, tiled=True, axis_...  9.5 us
    all_to_all x1, waiting for transfers between devices, per_device(): lax.all_to_all(pair, 'ma', split_axis=0, concat_axis=0, tiled=True, axis_...  8.61 us
    pallas_call x1, Pallas kernels, transform(): pl.pallas_call(body, out_shape=[jax.ShapeDtypeStruct((count // 2, 2 * GRO...  3.95 us
    pallas_call x1, Pallas kernels, project(): pl.pallas_call(body, out_shape=jax.ShapeDtypeStruct((shares, 2, padded(wi...  2.96 us
    pallas_call x1, Pallas kernels, factors(): pl.pallas_call(body, out_shape=[pltpu.VMEM((2, 2 * GROUPS, line), jnp.flo...  1.9 us
    ppermute x1, waiting for transfers between devices, per_device(): lax.ppermute(send, 'ma', [(slot, slot ^ 1) for slot in range(slots)])  1.83 us
    convert_element_type x1, other arithmetic, per_device(): pair = (keep + other).astype(jnp.bfloat16)  1.69 us
  transfers between devices with their start and end apart: 2, of which 2 were waited for; matrix products, arithmetic and copies ran while one was open for 0% of the time, Pallas kernels for 4%

profile of v2, /device:TPU:8, one launch (start us, length us, event | category | flops | bytes accessed | tf_op | source)
XLA Modules:
  0.0 44.3 jit_solution(3024487508602115010)
XLA Ops:
  0.0 0.0 copy-start.1
  0.0 0.0 copy-start
  0.0 3.9 %transform.1 = (f32[16,8,640]{2,1,0:T(8,128)}, f32[16,8,640]{2,1,0:T(8,128)}) custom-call(s32[1]{0:T(128)} %bitcast.slot_ref, s32[32]{0:T(128)} %refs_0_.1, bf16[2,2080,256]{2,1,0:T(8,128)(2,1)} %refs_1_.2), custom_call_target="tpu_custom_call" | custom-call | tf_op jit(solution)/shard_map/transform/pallas_call | solution.py:87
  4.0 0.1 collective-permute-start
  4.1 1.8 %collective-permute-done = f32[16,8,640]{2,1,0:T(8,128)S(1)} collective-permute-done((f32[16,8,640]{2,1,0:T(8,128)}, f32[16,8,640]{2,1,0:T(8,128)S(1)}, u32[]{:S(2)}, u32[]{:S(2)}) %collective-permute-start) | collective-permute-done | bytes 327712 | tf_op jit(solution)/shard_map/ppermute | solution.py:250
  5.9 1.7 %add_convert_fusion = bf16[16,8,640]{2,1,0:T(8,128)(2,1)} fusion(f32[16,8,640]{2,1,0:T(8,128)} %get-tuple-element.9, f32[16,8,640]{2,1,0:T(8,128)S(1)} %collective-permute-done), kind=kLoop, calls=%fused_computation | loop fusion | flops 163840 | bytes 819200 | tf_op jit(solution)/shard_map/convert_element_type | solution.py:251
  7.6 9.5 %all-to-all-start = ((bf16[16,8,640]{2,1,0:T(8,128)(2,1)}), bf16[16,8,640]{2,1,0:T(8,128)(2,1)S(1)}, u32[]{:S(2)}, u32[]{:S(2)}) async-start(bf16[16,8,640]{2,1,0:T(8,128)(2,1)} %add_convert_fusion), calls=%async_computation | async-start | bytes 327680 | tf_op jit(solution)/shard_map/all_to_all | solution.py:253
  17.1 0.0 copy-done.1
  17.1 0.0 copy-done
  17.1 1.9 %factors.1 = (f32[2,8,640]{2,1,0:T(8,128)S(1)}, bf16[1536,1000]{1,0:T(8,128)(2,1)S(1)}) custom-call(s32[2,2080]{1,0:T(2,128)S(1)} %bitcast.4, f32[2,1024]{1,0:T(2,128)S(1)} %copy-done.1, bf16[1,2,2080,1000]{3,2,1,0:T(8,128)(2,1)} %refs_3_.1), custom_call_target="tpu_custom_call" | custom-call | flops 51118080 | bytes 3088640 | tf_op jit(solution)/shard_map/factors/pallas_call | solution.py:155
  19.0 8.6 %all-to-all-done.refs_0_ = bf16[16,8,640]{2,1,0:T(8,128)(2,1)S(1)} async-done(((bf16[16,8,640]{2,1,0:T(8,128)(2,1)}), bf16[16,8,640]{2,1,0:T(8,128)(2,1)S(1)}, u32[]{:S(2)}, u32[]{:S(2)}) %all-to-all-start) | async-done | bytes 163872 | tf_op jit(solution)/shard_map/all_to_all | solution.py:253
  27.6 3.0 %project.1 = f32[8,2,128]{2,1,0:T(2,128)S(1)} custom-call(bf16[16,8,640]{2,1,0:T(8,128)(2,1)S(1)} %all-to-all-done.refs_0_, f32[2,8,640]{2,1,0:T(8,128)S(1)} %get-tuple-element.11.refs_1_, bf16[1536,1000]{1,0:T(8,128)(2,1)S(1)} %get-tuple-element.12.refs_2_, bf16[1,2,2080,1000]{3,2,1,0:T(8,128)(2,1)} %refs_3_.1), custom_call_target="tpu_custom_call" | custom-call | tf_op jit(solution)/shard_map/project/pallas_call | solution.py:228
  30.6 13.1 %all_to_all.10 = f32[8,2,128]{2,1,0:T(2,128)S(1)} all-to-all(f32[8,2,128]{2,1,0:T(2,128)S(1)} %project.1), channel_id=1, replica_groups=mesh['ma'=32,'bl'=8] {'bl'}, dimensions={0} | all-to-all | bytes 16384 | tf_op jit(solution)/shard_map/all_to_all | solution.py:256
  43.7 0.6 %reduce_sum.9 = f32[2,128]{1,0:T(2,128)} reduce(f32[8,2,128]{2,1,0:T(2,128)S(1)} %all_to_all.10, f32[]{:T(128)} %constant.7.clone.1), dimensions={0}, to_apply=%region_0.0 | reduce | flops 1792 | bytes 9220 | tf_op jit(solution)/shard_map/reduce_sum | solution.py:257
Async XLA Ops:
  0.0 17.1 %copy-start.1 = (f32[2,1024]{1,0:T(2,128)S(1)}, f32[2,1024]{1,0:T(2,128)}, u32[]{:S(2)}) copy-start(f32[2,1024]{1,0:T(2,128)} %refs_1_.3) | copy-start | bytes 24580
  0.0 17.1 %copy-start = (s32[2080,2]{0,1:T(2,128)S(1)}, s32[2080,2]{0,1:T(2,128)}, u32[]{:S(2)}) copy-start(s32[2080,2]{0,1:T(2,128)} %param.7) | copy-start | bytes 49924
  4.0 1.9 %collective-permute-start = (f32[16,8,640]{2,1,0:T(8,128)}, f32[16,8,640]{2,1,0:T(8,128)S(1)}, u32[]{:S(2)}, u32[]{:S(2)}) collective-permute-start(f32[16,8,640]{2,1,0:T(8,128)} %get-tuple-element.10), channel_id=1, source_target_pairs={{0,8},{8,0},{16,24},{24,16},{32,40},{40,32},{48,56},{56,48},{64,72... | collective-permute-start | bytes 983048 | tf_op jit(solution)/shard_map/ppermute | solution.py:250
  7.6 20.0 %all-to-all-start = ((bf16[16,8,640]{2,1,0:T(8,128)(2,1)}), bf16[16,8,640]{2,1,0:T(8,128)(2,1)S(1)}, u32[]{:S(2)}, u32[]{:S(2)}) async-start(bf16[16,8,640]{2,1,0:T(8,128)(2,1)} %add_convert_fusion), calls=%async_computation | async-start | bytes 327680 | tf_op jit(solution)/shard_map/all_to_all | solution.py:253

commit v3 on v2

--- a/solution.py
+++ b/solution.py
@@ -18,6 +18,10 @@
     return [(start, (starts[i + 1] if i + 1 < GROUPS else rows) - start) for i, start in enumerate(starts)]
 
 
+def rotated(count, first):
+    return [(first + i) % count for i in range(count)]
+
+
 def lane_pieces(size):
     return [(at, min(LANES, size - at)) for at in range(0, size, LANES)]
 
@@ -26,7 +30,7 @@
     return -(-size // LANES) * LANES
 
 
-def transform_kernel(spans, my_slot, m_ref, vis_ref, keep_ref, send_ref, held, lines, sems):
+def transform_kernel(spans, order, my_slot, m_ref, vis_ref, keep_ref, send_ref, held, lines, sems):
     copies = []
     for group, (start, size) in enumerate(spans):
         rows = pl.ds(start, size)
@@ -40,8 +44,8 @@
     row = lax.broadcasted_iota(jnp.int32, (count, LANES), 0)
     m_values = jnp.zeros((count, LANES), jnp.int32)
     for i in range(half):
-        m_values = jnp.where(row == i, m_ref[2 * i + parity] - count // 2, m_values)
-        m_values = jnp.where(row == half + i, m_ref[2 * i + 1 - parity] - count // 2, m_values)
+        m_values = jnp.where(row == i, m_ref[2 * order[i] + parity] - count // 2, m_values)
+        m_values = jnp.where(row == half + i, m_ref[2 * order[i] + 1 - parity] - count // 2, m_values)
     begin = my_slot * times
     scale = 1.0 / jnp.sqrt(jnp.float32(NT))
     cos_parts, sin_parts = [], []
@@ -75,18 +79,18 @@
         send_ref[:, :, piece * LANES:(piece + 1) * LANES] = block[half:]
 
 
-def transform(visibilities, m_order, slot):
+def transform(visibilities, m_order, slot, order):
     rows, times = visibilities.shape[1:]
     count = m_order.shape[0]
     spans = group_spans(rows)
     width = padded(max(size for _, size in spans))
 
     def body(slot_ref, *refs):
-        transform_kernel(spans, slot_ref[0], *refs)
+        transform_kernel(spans, order, slot_ref[0], *refs)
 
     return pl.pallas_call(
         body,
-        out_shape=[jax.ShapeDtypeStruct((count // 2, 2 * GROUPS, width), jnp.float32)] * 2,
+        out_shape=[pltpu.VMEM((count // 2, 2 * GROUPS, width), jnp.float32)] * 2,
         in_specs=[
             pl.BlockSpec(memory_space=pltpu.SMEM),
             pl.BlockSpec(memory_space=pltpu.SMEM),
@@ -173,7 +177,7 @@
     )(jnp.transpose(feed_pairs), feed_gains, pltpu.with_memory_space_constraint(beam_blocks, pltpu.HBM))
 
 
-def project_kernel(spans, shares, got_ref, factor_ref, early_ref, beam_ref, out_ref, held, sems):
+def project_kernel(spans, share_order, got_ref, factor_ref, early_ref, beam_ref, out_ref, held, sems):
     copies = {}
     for part in range(2):
         for group, (start, size) in enumerate(spans):
@@ -213,21 +217,21 @@
         )
     answer = jnp.concatenate([sums[0][0] + sums[1][1], sums[0][1] - sums[1][0]], axis=0)
     width = answer.shape[1]
-    share = width // shares
-    for k in range(shares):
-        out_ref[k, :, :share] = answer[:, k * share:(k + 1) * share]
-
-
-def project(got, factor, early, beam_blocks, shares):
+    share = width // len(share_order)
+    for slab, k in enumerate(share_order):
+        out_ref[slab, :, :share] = answer[:, k * share:(k + 1) * share]
+
+
+def project(got, factor, early, beam_blocks, share_order):
     rows, width = beam_blocks.shape[2:]
     spans = group_spans(rows)
 
     def body(*refs):
-        project_kernel(spans, shares, *refs)
+        project_kernel(spans, share_order, *refs)
 
     return pl.pallas_call(
         body,
-        out_shape=jax.ShapeDtypeStruct((shares, 2, padded(width // shares)), jnp.float32),
+        out_shape=jax.ShapeDtypeStruct((len(share_order), 2, padded(width // len(share_order))), jnp.float32),
         in_specs=[pl.BlockSpec(memory_space=pltpu.VMEM)] * 3 + [pl.BlockSpec(memory_space=pltpu.HBM)],
         out_specs=pl.BlockSpec(memory_space=pltpu.VMEM),
         scratch_shapes=[
@@ -246,14 +250,18 @@
     shares = lax.axis_size("bl")
     slots = lax.axis_size("ma")
     share_width = beam_blocks.shape[3] // shares
-    keep, send = transform(visibilities, m_order, lax.axis_index("ma"))
+    order = rotated(slots // 2, slots // 4)
+    keep, send = transform(visibilities, m_order, lax.axis_index("ma"), order)
     other = lax.ppermute(send, "ma", [(slot, slot ^ 1) for slot in range(slots)])
     pair = (keep + other).astype(jnp.bfloat16)
-    same_core = [[2 * i + parity for i in range(slots // 2)] for parity in range(2)]
+    same_core = [[2 * i + parity for i in order] for parity in range(2)]
     got = lax.all_to_all(pair, "ma", split_axis=0, concat_axis=0, tiled=True, axis_index_groups=same_core)
     factor, early = factors(feed_pairs, feed_gains, beam_blocks)
-    partial_modes = project(got, factor, early, beam_blocks, shares)
-    parts = lax.all_to_all(partial_modes, "bl", split_axis=0, concat_axis=0, tiled=True)
+    share_order = rotated(shares, shares // 2 + 1)
+    partial_modes = project(got, factor, early, beam_blocks, share_order)
+    parts = lax.all_to_all(
+        partial_modes, "bl", split_axis=0, concat_axis=0, tiled=True, axis_index_groups=[share_order]
+    )
     return jnp.sum(parts, axis=0)[:, None, :share_width]
 
 

time: 44.6 us -> 36.6 us (0.82)
  waiting for transfers between devices: 10.4 us -> 5.29 us
  blocking collectives: 13.1 us -> 10.2 us
  starting transfers between devices: 9.59 us -> 11.4 us
  other arithmetic: 2.27 us -> 1.27 us
  Pallas kernels: 8.81 us -> 7.98 us
    all_to_all x1, waiting for transfers between devices: 8.61 us -> 3.68 us  [per_device(): lax.all_to_all(pair, 'ma', split_axis=0, concat_axis=0, tiled=True, axis_...]
    all_to_all x1, blocking collectives: 13.1 us -> 10.2 us  [per_device(): lax.all_to_all(partial_modes, 'bl', split_axis=0, concat_axis=0, tiled=Tr...]
    all_to_all x1, starting transfers between devices: 9.5 us -> 11.3 us  [per_device(): lax.all_to_all(pair, 'ma', split_axis=0, concat_axis=0, tiled=True, axis_...]
    convert_element_type x1, other arithmetic: 1.69 us -> 0.69 us  [per_device(): pair = (keep + other).astype(jnp.bfloat16)]
    pallas_call x2, Pallas kernels: 6.91 us -> 6.08 us  [the longest x1 3.11 us: transform(): pl.pallas_call(body, out_shape=[pltpu.VMEM((count // 2, 2 * GROUPS, width...]
  transfers between devices with their start and end apart: 2 -> 2, of which waited for: 2 -> 2; matrix products, arithmetic and copies ran while one was open for 0% -> 0% of each run, Pallas kernels for 4% -> 5%
where the time goes in v3:
time: 36.6 us; the launch traced here: 36.2 us
  starting transfers between devices  11.4 us (31%)
  blocking collectives  10.2 us (28%)
  Pallas kernels  7.98 us (22%)
  waiting for transfers between devices  5.29 us (14%)
  other arithmetic  1.27 us (3%)
    all_to_all x1, starting transfers between devices, per_device(): lax.all_to_all(pair, 'ma', split_axis=0, concat_axis=0, tiled=True, axis_...  11.3 us
    all_to_all x1, blocking collectives, per_device(): lax.all_to_all(partial_modes, 'bl', split_axis=0, concat_axis=0, tiled=Tr...  10.2 us
    all_to_all x1, waiting for transfers between devices, per_device(): lax.all_to_all(pair, 'ma', split_axis=0, concat_axis=0, tiled=True, axis_...  3.68 us
    pallas_call x1, Pallas kernels, transform(): pl.pallas_call(body, out_shape=[pltpu.VMEM((count // 2, 2 * GROUPS, width...  3.11 us
    pallas_call x1, Pallas kernels, project(): pl.pallas_call(body, out_shape=jax.ShapeDtypeStruct((len(share_order), 2,...  2.96 us
    pallas_call x1, Pallas kernels, factors(): pl.pallas_call(body, out_shape=[pltpu.VMEM((2, 2 * GROUPS, line), jnp.flo...  1.9 us
    ppermute x1, waiting for transfers between devices, per_device(): lax.ppermute(send, 'ma', [(slot, slot ^ 1) for slot in range(slots)])  1.62 us
  transfers between devices with their start and end apart: 2, of which 2 were waited for; matrix products, arithmetic and copies ran while one was open for 0% of the time, Pallas kernels for 5%

profile of v3, /device:TPU:8, one launch (start us, length us, event | category | flops | bytes accessed | tf_op | source)
XLA Modules:
  0.0 36.2 jit_solution(1602561386983190263)
XLA Ops:
  0.0 0.0 copy-start.1
  0.0 0.0 copy-start
  0.0 3.1 %transform.1 = (f32[16,8,640]{2,1,0:T(8,128)S(1)}, f32[16,8,640]{2,1,0:T(8,128)S(1)}) custom-call(s32[1]{0:T(128)} %bitcast.slot_ref, s32[32]{0:T(128)} %refs_0_.1, bf16[2,2080,256]{2,1,0:T(8,128)(2,1)} %refs_1_.2), custom_call_target="tpu_custom_call" | custom-call | tf_op jit(solution)/shard_map/transform/pallas_call | solution.py:91
  3.1 0.1 collective-permute-start
  3.2 1.6 %collective-permute-done = f32[16,8,640]{2,1,0:T(8,128)S(1)} collective-permute-done((f32[16,8,640]{2,1,0:T(8,128)S(1)}, f32[16,8,640]{2,1,0:T(8,128)S(1)}, u32[]{:S(2)}, u32[]{:S(2)}) %collective-permute-start) | collective-permute-done | bytes 327712 | tf_op jit(solution)/shard_map/ppermute | solution.py:255
  4.8 0.7 %add_convert_fusion = bf16[16,8,640]{2,1,0:T(8,128)(2,1)} fusion(f32[16,8,640]{2,1,0:T(8,128)S(1)} %get-tuple-element.9, f32[16,8,640]{2,1,0:T(8,128)S(1)} %collective-permute-done), kind=kLoop, calls=%fused_computation | loop fusion | flops 163840 | bytes 819200 | tf_op jit(solution)/shard_map/convert_element_type | solution.py:256
  5.5 11.3 %all-to-all-start = ((bf16[16,8,640]{2,1,0:T(8,128)(2,1)}), bf16[16,8,640]{2,1,0:T(8,128)(2,1)S(1)}, u32[]{:S(2)}, u32[]{:S(2)}) async-start(bf16[16,8,640]{2,1,0:T(8,128)(2,1)} %add_convert_fusion), calls=%async_computation | async-start | bytes 327680 | tf_op jit(solution)/shard_map/all_to_all | solution.py:258
  16.9 0.0 copy-done.1
  16.9 0.0 copy-done
  16.9 1.9 %factors.1 = (f32[2,8,640]{2,1,0:T(8,128)S(1)}, bf16[1536,1000]{1,0:T(8,128)(2,1)S(1)}) custom-call(s32[2,2080]{1,0:T(2,128)S(1)} %bitcast.4, f32[2,1024]{1,0:T(2,128)S(1)} %copy-done.1, bf16[1,2,2080,1000]{3,2,1,0:T(8,128)(2,1)} %refs_3_.1), custom_call_target="tpu_custom_call" | custom-call | flops 51118080 | bytes 3088640 | tf_op jit(solution)/shard_map/factors/pallas_call | solution.py:159
  18.8 3.7 %all-to-all-done.refs_0_ = bf16[16,8,640]{2,1,0:T(8,128)(2,1)S(1)} async-done(((bf16[16,8,640]{2,1,0:T(8,128)(2,1)}), bf16[16,8,640]{2,1,0:T(8,128)(2,1)S(1)}, u32[]{:S(2)}, u32[]{:S(2)}) %all-to-all-start) | async-done | bytes 163872 | tf_op jit(solution)/shard_map/all_to_all | solution.py:258
  22.5 3.0 %project.1 = f32[8,2,128]{2,1,0:T(2,128)S(1)} custom-call(bf16[16,8,640]{2,1,0:T(8,128)(2,1)S(1)} %all-to-all-done.refs_0_, f32[2,8,640]{2,1,0:T(8,128)S(1)} %get-tuple-element.11.refs_1_, bf16[1536,1000]{1,0:T(8,128)(2,1)S(1)} %get-tuple-element.12.refs_2_, bf16[1,2,2080,1000]{3,2,1,0:T(8,128)(2,1)} %refs_3_.1), custom_call_target="tpu_custom_call" | custom-call | tf_op jit(solution)/shard_map/project/pallas_call | solution.py:232
  25.4 10.2 %all_to_all.10 = f32[8,2,128]{2,1,0:T(2,128)S(1)} all-to-all(f32[8,2,128]{2,1,0:T(2,128)S(1)} %project.1), channel_id=1, replica_groups={{5,6,7,0,1,2,3,4},{13,14,15,8,9,10,11,12},{21,22,23,16,17,18,19,20},{29..., dimensions={0} | all-to-all | bytes 16384 | tf_op jit(solution)/shard_map/all_to_all | solution.py:262
  35.6 0.6 %reduce_sum.9 = f32[2,128]{1,0:T(2,128)} reduce(f32[8,2,128]{2,1,0:T(2,128)S(1)} %all_to_all.10, f32[]{:T(128)} %constant.7.clone.1), dimensions={0}, to_apply=%region_0.0 | reduce | flops 1792 | bytes 9220 | tf_op jit(solution)/shard_map/reduce_sum | solution.py:265
Async XLA Ops:
  0.0 16.9 %copy-start.1 = (f32[2,1024]{1,0:T(2,128)S(1)}, f32[2,1024]{1,0:T(2,128)}, u32[]{:S(2)}) copy-start(f32[2,1024]{1,0:T(2,128)} %refs_1_.3) | copy-start | bytes 24580
  0.0 16.9 %copy-start = (s32[2080,2]{0,1:T(2,128)S(1)}, s32[2080,2]{0,1:T(2,128)}, u32[]{:S(2)}) copy-start(s32[2080,2]{0,1:T(2,128)} %param.7) | copy-start | bytes 49924
  3.1 1.7 %collective-permute-start = (f32[16,8,640]{2,1,0:T(8,128)S(1)}, f32[16,8,640]{2,1,0:T(8,128)S(1)}, u32[]{:S(2)}, u32[]{:S(2)}) collective-permute-start(f32[16,8,640]{2,1,0:T(8,128)S(1)} %get-tuple-element.10), channel_id=1, source_target_pairs={{0,8},{8,0},{16,24},{24,16},{32,40},{40,32},{48,56},{56,48},{64,72... | collective-permute-start | bytes 983048 | tf_op jit(solution)/shard_map/ppermute | solution.py:255
  5.5 16.9 %all-to-all-start = ((bf16[16,8,640]{2,1,0:T(8,128)(2,1)}), bf16[16,8,640]{2,1,0:T(8,128)(2,1)S(1)}, u32[]{:S(2)}, u32[]{:S(2)}) async-start(bf16[16,8,640]{2,1,0:T(8,128)(2,1)} %add_convert_fusion), calls=%async_computation | async-start | bytes 327680 | tf_op jit(solution)/shard_map/all_to_all | solution.py:258

commit v4 on v3

--- a/solution.py
+++ b/solution.py
@@ -7,9 +7,10 @@
 
 NT = 8192
 GROUPS = 4
-EARLY = 3
 LANES = 128
 MIB = 1024 * 1024
+FIRST_ROWS = 2080
+SECOND_ROWS = 1536
 
 
 def group_spans(rows):
@@ -30,13 +31,20 @@
     return -(-size // LANES) * LANES
 
 
-def transform_kernel(spans, order, my_slot, m_ref, vis_ref, keep_ref, send_ref, held, lines, sems):
+def transform_kernel(
+    spans, order, my_slot, given_m, vis_ref, beam_ref, keep_ref, send_ref, early_ref, held, lines, m_ref, sems
+):
+    fetch_m = pltpu.make_async_copy(given_m, m_ref, sems.at[GROUPS + 1])
+    fetch_m.start()
     copies = []
     for group, (start, size) in enumerate(spans):
         rows = pl.ds(start, size)
         copy = pltpu.make_async_copy(vis_ref.at[:, rows, :], held.at[:, rows, :], sems.at[group])
         copy.start()
         copies.append(copy)
+    early = pltpu.make_async_copy(beam_ref.at[pl.ds(0, early_ref.shape[0]), :], early_ref, sems.at[GROUPS])
+    early.start()
+    fetch_m.wait()
     count = m_ref.shape[0]
     half = count // 2
     times = vis_ref.shape[2]
@@ -77,9 +85,10 @@
         block = lines[piece].reshape(count, 2 * GROUPS, LANES)
         keep_ref[:, :, piece * LANES:(piece + 1) * LANES] = block[:half]
         send_ref[:, :, piece * LANES:(piece + 1) * LANES] = block[half:]
-
-
-def transform(visibilities, m_order, slot, order):
+    early.wait()
+
+
+def transform(visibilities, beam, m_order, slot, order):
     rows, times = visibilities.shape[1:]
     count = m_order.shape[0]
     spans = group_spans(rows)
@@ -90,20 +99,27 @@
 
     return pl.pallas_call(
         body,
-        out_shape=[pltpu.VMEM((count // 2, 2 * GROUPS, width), jnp.float32)] * 2,
+        out_shape=[pltpu.VMEM((count // 2, 2 * GROUPS, width), jnp.float32)] * 2
+        + [pltpu.VMEM((FIRST_ROWS, beam.shape[1]), jnp.bfloat16)],
         in_specs=[
             pl.BlockSpec(memory_space=pltpu.SMEM),
-            pl.BlockSpec(memory_space=pltpu.SMEM),
-            pl.BlockSpec(memory_space=pl.ANY),
+            pl.BlockSpec(memory_space=pltpu.HBM),
+            pl.BlockSpec(memory_space=pltpu.HBM),
+            pl.BlockSpec(memory_space=pltpu.HBM),
         ],
-        out_specs=[pl.BlockSpec(memory_space=pltpu.VMEM)] * 2,
+        out_specs=[pl.BlockSpec(memory_space=pltpu.VMEM)] * 3,
         scratch_shapes=[
             pltpu.VMEM((2, rows, times), jnp.bfloat16),
             pltpu.VMEM((width // LANES, count * 2 * GROUPS, LANES), jnp.float32),
-            pltpu.SemaphoreType.DMA((GROUPS,)),
+            pltpu.SMEM((count,), jnp.int32),
+            pltpu.SemaphoreType.DMA((GROUPS + 2,)),
         ],
+        compiler_params=pltpu.CompilerParams(vmem_limit_bytes=24 * MIB),
         name="transform",
-    )(slot.reshape(1), m_order, pltpu.with_memory_space_constraint(visibilities, pltpu.HBM))
+    )(
+        slot.reshape(1),
+        *(pltpu.with_memory_space_constraint(given, pltpu.HBM) for given in (m_order, visibilities, beam)),
+    )
 
 
 def three_pieces(value):
@@ -114,9 +130,16 @@
     return [first, second, third]
 
 
-def factor_kernel(spans, pairs_ref, gains_ref, beam_ref, out_ref, held_ref, sem):
-    copy = pltpu.make_async_copy(beam_ref.at[0, 0, pl.ds(0, held_ref.shape[0]), :], held_ref, sem)
-    copy.start()
+def factor_kernel(spans, given_pairs, given_gains, beam_ref, out_ref, early_ref, pairs_ref, gains_ref, sems):
+    fetches = [
+        pltpu.make_async_copy(given_pairs, pairs_ref, sems.at[0]),
+        pltpu.make_async_copy(given_gains, gains_ref, sems.at[1]),
+        pltpu.make_async_copy(beam_ref.at[pl.ds(FIRST_ROWS, early_ref.shape[0]), :], early_ref, sems.at[2]),
+    ]
+    for fetch in fetches:
+        fetch.start()
+    for fetch in fetches[:2]:
+        fetch.wait()
     feeds = gains_ref.shape[1]
     tiles = feeds // LANES
     table = jnp.concatenate(
@@ -145,11 +168,11 @@
         out_ref[0, GROUPS + group:GROUPS + group + 1, :size] = factor_re
         out_ref[1, group:group + 1, :size] = -factor_im
         out_ref[1, GROUPS + group:GROUPS + group + 1, :size] = factor_im
-    copy.wait()
-
-
-def factors(feed_pairs, feed_gains, beam_blocks):
-    rows, width = beam_blocks.shape[2:]
+    fetches[2].wait()
+
+
+def factors(feed_pairs, feed_gains, beam):
+    rows, width = feed_pairs.shape[0], beam.shape[1]
     spans = group_spans(rows)
     line = padded(max(size for _, size in spans))
 
@@ -160,36 +183,36 @@
         body,
         out_shape=[
             pltpu.VMEM((2, 2 * GROUPS, line), jnp.float32),
-            pltpu.VMEM((spans[EARLY][0], width), jnp.bfloat16),
+            pltpu.VMEM((SECOND_ROWS, width), jnp.bfloat16),
         ],
-        in_specs=[
-            pl.BlockSpec(memory_space=pltpu.VMEM),
-            pl.BlockSpec(memory_space=pltpu.VMEM),
-            pl.BlockSpec(memory_space=pltpu.HBM),
+        in_specs=[pl.BlockSpec(memory_space=pltpu.HBM)] * 3,
+        out_specs=[pl.BlockSpec(memory_space=pltpu.VMEM)] * 2,
+        scratch_shapes=[
+            pltpu.VMEM(feed_pairs.shape[::-1], jnp.int32),
+            pltpu.VMEM(feed_gains.shape, jnp.float32),
+            pltpu.SemaphoreType.DMA((3,)),
         ],
-        out_specs=[pl.BlockSpec(memory_space=pltpu.VMEM)] * 2,
-        scratch_shapes=[pltpu.SemaphoreType.DMA],
         cost_estimate=pl.CostEstimate(
-            flops=2 * 2 * rows * 48 * 128, bytes_accessed=2 * spans[EARLY][0] * width + 8 * rows, transcendentals=0
+            flops=2 * 2 * rows * 48 * 128, bytes_accessed=2 * SECOND_ROWS * width + 8 * rows, transcendentals=0
         ),
         compiler_params=pltpu.CompilerParams(vmem_limit_bytes=16 * MIB),
         name="factors",
-    )(jnp.transpose(feed_pairs), feed_gains, pltpu.with_memory_space_constraint(beam_blocks, pltpu.HBM))
-
-
-def project_kernel(spans, share_order, got_ref, factor_ref, early_ref, beam_ref, out_ref, held, sems):
-    copies = {}
-    for part in range(2):
-        for group, (start, size) in enumerate(spans):
-            if part == 0 and group < EARLY:
-                continue
-            rows = pl.ds(start, size)
-            copies[part, group] = pltpu.make_async_copy(
-                beam_ref.at[0, part, rows, :],
-                held.at[pl.ds(part * spans[-1][1] + (start if part else 0), size), :],
-                sems.at[part * GROUPS + group],
-            )
-            copies[part, group].start()
+    )(
+        *(
+            pltpu.with_memory_space_constraint(given, pltpu.HBM)
+            for given in (jnp.transpose(feed_pairs), feed_gains, beam)
+        )
+    )
+
+
+def project_kernel(spans, share_order, got_ref, factor_ref, first_ref, second_ref, beam_ref, out_ref, last_ref, sem):
+    places = []
+    begin = 0
+    for ref in (first_ref, second_ref, last_ref):
+        places.append((begin, ref))
+        begin += ref.shape[0]
+    late = pltpu.make_async_copy(beam_ref.at[pl.ds(places[-1][0], last_ref.shape[0]), :], last_ref, sem)
+    late.start()
     total = got_ref[0].astype(jnp.float32)
     for source in range(1, got_ref.shape[0]):
         total += got_ref[source].astype(jnp.float32)
@@ -201,16 +224,22 @@
     row_group = jnp.bitwise_and(lax.broadcasted_iota(jnp.int32, rows16.shape, 0), GROUPS - 1)
     lefts = [jnp.where(row_group == group, rows16, 0.0).astype(jnp.bfloat16) for group in range(GROUPS)]
     sums = []
+    waited = False
     for part in range(2):
         value = None
         for group, (start, size) in enumerate(spans):
-            if (part, group) in copies:
-                copies[part, group].wait()
-                right = held[pl.ds(part * spans[-1][1] + (start if part else 0), size), :]
-            else:
-                right = early_ref[pl.ds(start, size), :]
-            term = jnp.dot(lefts[group][:, :size], right, preferred_element_type=jnp.float32)
-            value = term if value is None else value + term
+            row = part * (spans[-1][0] + spans[-1][1]) + start
+            for begin, ref in places:
+                low = max(row, begin)
+                count = min(row + size, begin + ref.shape[0]) - low
+                if count <= 0:
+                    continue
+                if ref is last_ref and not waited:
+                    late.wait()
+                    waited = True
+                left = lefts[group][:, low - row:low - row + count]
+                term = jnp.dot(left, ref[pl.ds(low - begin, count), :], preferred_element_type=jnp.float32)
+                value = term if value is None else value + term
         value = value[:2 * GROUPS] + value[2 * GROUPS:]
         sums.append(
             [jnp.sum(value[piece * GROUPS:(piece + 1) * GROUPS], axis=0, keepdims=True) for piece in range(2)]
@@ -222,9 +251,9 @@
         out_ref[slab, :, :share] = answer[:, k * share:(k + 1) * share]
 
 
-def project(got, factor, early, beam_blocks, share_order):
-    rows, width = beam_blocks.shape[2:]
-    spans = group_spans(rows)
+def project(got, factor, first, second, beam, share_order):
+    rows, width = beam.shape
+    spans = group_spans(rows // 2)
 
     def body(*refs):
         project_kernel(spans, share_order, *refs)
@@ -232,17 +261,14 @@
     return pl.pallas_call(
         body,
         out_shape=jax.ShapeDtypeStruct((len(share_order), 2, padded(width // len(share_order))), jnp.float32),
-        in_specs=[pl.BlockSpec(memory_space=pltpu.VMEM)] * 3 + [pl.BlockSpec(memory_space=pltpu.HBM)],
+        in_specs=[pl.BlockSpec(memory_space=pltpu.VMEM)] * 4 + [pl.BlockSpec(memory_space=pltpu.HBM)],
         out_specs=pl.BlockSpec(memory_space=pltpu.VMEM),
-        scratch_shapes=[
-            pltpu.VMEM((spans[-1][1] + rows, width), jnp.bfloat16),
-            pltpu.SemaphoreType.DMA((2 * GROUPS,)),
-        ],
-        compiler_params=pltpu.CompilerParams(vmem_limit_bytes=24 * MIB),
+        scratch_shapes=[pltpu.VMEM((rows - FIRST_ROWS - SECOND_ROWS, width), jnp.bfloat16), pltpu.SemaphoreType.DMA],
+        compiler_params=pltpu.CompilerParams(vmem_limit_bytes=16 * MIB),
         name="project",
     )(
-        *(pltpu.with_memory_space_constraint(held, pltpu.VMEM) for held in (got, factor, early)),
-        pltpu.with_memory_space_constraint(beam_blocks, pltpu.HBM),
+        *(pltpu.with_memory_space_constraint(held, pltpu.VMEM) for held in (got, factor, first, second)),
+        pltpu.with_memory_space_constraint(beam, pltpu.HBM),
     )
 
 
@@ -251,14 +277,16 @@
     slots = lax.axis_size("ma")
     share_width = beam_blocks.shape[3] // shares
     order = rotated(slots // 2, slots // 4)
-    keep, send = transform(visibilities, m_order, lax.axis_index("ma"), order)
+    beam = beam_blocks.reshape(2 * beam_blocks.shape[2], beam_blocks.shape[3])
+    keep, send, first = transform(visibilities, beam, m_order, lax.axis_index("ma"), order)
+    send, feed_gains = lax.optimization_barrier((send, feed_gains))
+    factor, second = factors(feed_pairs, feed_gains, beam)
     other = lax.ppermute(send, "ma", [(slot, slot ^ 1) for slot in range(slots)])
-    pair = (keep + other).astype(jnp.bfloat16)
+    pair, factor = lax.optimization_barrier(((keep + other).astype(jnp.bfloat16), factor))
     same_core = [[2 * i + parity for i in order] for parity in range(2)]
     got = lax.all_to_all(pair, "ma", split_axis=0, concat_axis=0, tiled=True, axis_index_groups=same_core)
-    factor, early = factors(feed_pairs, feed_gains, beam_blocks)
     share_order = rotated(shares, shares // 2 + 1)
-    partial_modes = project(got, factor, early, beam_blocks, share_order)
+    partial_modes = project(got, factor, first, second, beam, share_order)
     parts = lax.all_to_all(
         partial_modes, "bl", split_axis=0, concat_axis=0, tiled=True, axis_index_groups=[share_order]
     )

time: 36.6 us -> 34.8 us (0.951)
  blocking collectives: 10.2 us -> 27.3 us
  starting transfers between devices: 11.4 us -> 0.09 us
  waiting for transfers between devices: 5.29 us -> 0.01 us
  Pallas kernels: 7.98 us -> 6.49 us
  other arithmetic: 1.27 us -> 0.63 us
    all_to_all x0 -> x1, blocking collectives: none -> 17.1 us  [per_device(): lax.all_to_all(pair, 'ma', split_axis=0, concat_axis=0, tiled=True, axis_...]
    all_to_all x1 -> x0, starting transfers between devices: 11.3 us -> none  [per_device(): lax.all_to_all(pair, 'ma', split_axis=0, concat_axis=0, tiled=True, axis_...]
    all_to_all x1 -> x0, waiting for transfers between devices: 3.68 us -> none  [per_device(): lax.all_to_all(pair, 'ma', split_axis=0, concat_axis=0, tiled=True, axis_...]
    ppermute x1, waiting for transfers between devices: 1.62 us -> 0.01 us  [per_device(): lax.ppermute(send, 'ma', [(slot, slot ^ 1) for slot in range(slots)])]
    pallas_call x1, Pallas kernels: 2.96 us -> 1.62 us  [project(): pl.pallas_call(body, out_shape=jax.ShapeDtypeStruct((len(share_order), 2,...]
    convert_element_type x1, other arithmetic: 0.69 us -> 0.05 us  [per_device(): (keep + other).astype(jnp.bfloat16)]
  transfers between devices with their start and end apart: 2 -> 1, of which waited for: 2 -> 0; matrix products, arithmetic and copies ran while one was open for 0% -> 0% of each run, Pallas kernels for 5% -> 6%
where the time goes in v4:
time: 34.8 us; the launch traced here: 34.5 us
  blocking collectives  27.3 us (78%)
  Pallas kernels  6.49 us (19%)
  other arithmetic  0.63 us (2%)
    all_to_all x1, blocking collectives, per_device(): lax.all_to_all(pair, 'ma', split_axis=0, concat_axis=0, tiled=True, axis_...  17.1 us
    all_to_all x1, blocking collectives, per_device(): lax.all_to_all(partial_modes, 'bl', split_axis=0, concat_axis=0, tiled=Tr...  10.2 us
    pallas_call x1, Pallas kernels, transform(): pl.pallas_call(body, out_shape=[pltpu.VMEM((count // 2, 2 * GROUPS, width...  2.92 us
    pallas_call x1, Pallas kernels, factors(): pl.pallas_call(body, out_shape=[pltpu.VMEM((2, 2 * GROUPS, line), jnp.flo...  1.95 us
    pallas_call x1, Pallas kernels, project(): pl.pallas_call(body, out_shape=jax.ShapeDtypeStruct((len(share_order), 2,...  1.62 us
  transfers between devices with their start and end apart: 1, of which 0 were waited for; matrix products, arithmetic and copies ran while one was open for 0% of the time, Pallas kernels for 6%

profile of v4, /device:TPU:8, one launch (start us, length us, event | category | flops | bytes accessed | tf_op | source)
XLA Modules:
  0.0 34.5 jit_solution(13536743352959297186)
XLA Ops:
  0.0 2.9 %transform.1 = (f32[16,8,640]{2,1,0:T(8,128)S(1)}, f32[16,8,640]{2,1,0:T(8,128)S(1)}, bf16[2080,1000]{1,0:T(8,128)(2,1)S(1)}) custom-call(s32[1]{0:T(128)} %bitcast.slot_ref, s32[32]{0:T(128)} %refs_0_.1, bf16[2,2080,256]{2,1,0:T(8,128)(2,1)} %refs_1_.1, bf16[4160,1000]{1,0:T(8,128)(2,1)} %bitcast.5), custom_call_target="tpu_custom_call" | custom-call | tf_op jit(solution)/shard_map/transform/pallas_call | solution.py:100
  2.9 0.1 collective-permute-start
  3.0 2.0 %factors.1 = (f32[2,8,640]{2,1,0:T(8,128)S(1)}, bf16[1536,1000]{1,0:T(8,128)(2,1)S(1)}) custom-call(s32[2,2080]{1,0:T(2,128)} %bitcast.8, f32[2,1024]{1,0:T(2,128)} %refs_1_.2, bf16[4160,1000]{1,0:T(8,128)(2,1)} %bitcast.6), custom_call_target="tpu_custom_call" | custom-call | flops 51118080 | bytes 3088640 | tf_op jit(solution)/shard_map/factors/pallas_call | solution.py:182
  5.0 0.0 collective-permute-done
  5.0 17.1 %all_to_all.10.refs_0_ = bf16[16,8,640]{2,1,0:T(8,128)(2,1)S(1)} all-to-all(bf16[16,8,640]{2,1,0:T(8,128)(2,1)S(1)} %add_convert_fusion), channel_id=1, replica_groups={{128,144,160,176,192,208,224,240,0,16,32,48,64,80,96,112},{136,152,168,..., dimensions={0} | all-to-all | bytes 327680 | tf_op jit(solution)/shard_map/all_to_all | solution.py:287
  22.1 1.6 %project.1 = f32[8,2,128]{2,1,0:T(2,128)S(1)} custom-call(bf16[16,8,640]{2,1,0:T(8,128)(2,1)S(1)} %all_to_all.10.refs_0_, f32[2,8,640]{2,1,0:T(8,128)S(1)} %get-tuple-element.20.refs_1_, bf16[2080,1000]{1,0:T(8,128)(2,1)S(1)} %get-tuple-element.21.refs_2_, bf16[1536,1000]{1,0:T(8,128)(2,1)S(1)} %get-tuple-element.22.refs_3_, bf16[4160,1000]{1,0:T(8,128)(2,1)} %bitcast.7), custom_call_target="tpu_custom_call" | custom-call | tf_op jit(solution)/shard_map/project/pallas_call | solution.py:261
  23.8 10.2 %all_to_all.11 = f32[8,2,128]{2,1,0:T(2,128)S(1)} all-to-all(f32[8,2,128]{2,1,0:T(2,128)S(1)} %project.1), channel_id=1, replica_groups={{5,6,7,0,1,2,3,4},{13,14,15,8,9,10,11,12},{21,22,23,16,17,18,19,20},{29..., dimensions={0} | all-to-all | bytes 16384 | tf_op jit(solution)/shard_map/all_to_all | solution.py:290
  33.9 0.6 %reduce_sum.9 = f32[2,128]{1,0:T(2,128)} reduce(f32[8,2,128]{2,1,0:T(2,128)S(1)} %all_to_all.11, f32[]{:T(128)} %constant.7.clone.1), dimensions={0}, to_apply=%region_0.0 | reduce | flops 1792 | bytes 9220 | tf_op jit(solution)/shard_map/reduce_sum | solution.py:293
  (1 shorter events, 0.0 us)
Async XLA Ops:
  2.9 2.1 %collective-permute-start = (f32[16,8,640]{2,1,0:T(8,128)S(1)}, f32[16,8,640]{2,1,0:T(8,128)S(1)}, u32[]{:S(2)}, u32[]{:S(2)}) collective-permute-start(f32[16,8,640]{2,1,0:T(8,128)S(1)} %get-tuple-element.16), channel_id=1, source_target_pairs={{0,8},{8,0},{16,24},{24,16},{32,40},{40,32},{48,56},{56,48},{64,72... | collective-permute-start | bytes 983048 | tf_op jit(solution)/shard_map/ppermute | solution.py:284

commit v5 on v4

--- a/solution.py
+++ b/solution.py
@@ -9,8 +9,6 @@
 GROUPS = 4
 LANES = 128
 MIB = 1024 * 1024
-FIRST_ROWS = 2080
-SECOND_ROWS = 1536
 
 
 def group_spans(rows):
@@ -100,7 +98,7 @@
     return pl.pallas_call(
         body,
         out_shape=[pltpu.VMEM((count // 2, 2 * GROUPS, width), jnp.float32)] * 2
-        + [pltpu.VMEM((FIRST_ROWS, beam.shape[1]), jnp.bfloat16)],
+        + [pltpu.VMEM((beam.shape[0] // 2, beam.shape[1]), jnp.bfloat16)],
         in_specs=[
             pl.BlockSpec(memory_space=pltpu.SMEM),
             pl.BlockSpec(memory_space=pltpu.HBM),
@@ -130,15 +128,22 @@
     return [first, second, third]
 
 
-def factor_kernel(spans, given_pairs, given_gains, beam_ref, out_ref, early_ref, pairs_ref, gains_ref, sems):
+def factor_kernel(
+    spans, eager, given_pairs, given_gains, beam_ref, out_ref, early_ref, pairs_ref, gains_ref, sems
+):
     fetches = [
         pltpu.make_async_copy(given_pairs, pairs_ref, sems.at[0]),
         pltpu.make_async_copy(given_gains, gains_ref, sems.at[1]),
-        pltpu.make_async_copy(beam_ref.at[pl.ds(FIRST_ROWS, early_ref.shape[0]), :], early_ref, sems.at[2]),
     ]
     for fetch in fetches:
         fetch.start()
-    for fetch in fetches[:2]:
+    early = pltpu.make_async_copy(beam_ref.at[pl.ds(early_ref.shape[0], early_ref.shape[0]), :], early_ref, sems.at[2])
+
+    @pl.when(eager)
+    def start_early():
+        early.start()
+
+    for fetch in fetches:
         fetch.wait()
     feeds = gains_ref.shape[1]
     tiles = feeds // LANES
@@ -168,24 +173,27 @@
         out_ref[0, GROUPS + group:GROUPS + group + 1, :size] = factor_re
         out_ref[1, group:group + 1, :size] = -factor_im
         out_ref[1, GROUPS + group:GROUPS + group + 1, :size] = factor_im
-    fetches[2].wait()
-
-
-def factors(feed_pairs, feed_gains, beam):
+
+    @pl.when(eager)
+    def finish_early():
+        early.wait()
+
+
+def factors(feed_pairs, feed_gains, beam, slot, eager_slots):
     rows, width = feed_pairs.shape[0], beam.shape[1]
     spans = group_spans(rows)
     line = padded(max(size for _, size in spans))
 
-    def body(*refs):
-        factor_kernel(spans, *refs)
+    def body(slot_ref, *refs):
+        factor_kernel(spans, slot_ref[0] < eager_slots, *refs)
 
     return pl.pallas_call(
         body,
         out_shape=[
             pltpu.VMEM((2, 2 * GROUPS, line), jnp.float32),
-            pltpu.VMEM((SECOND_ROWS, width), jnp.bfloat16),
-        ],
-        in_specs=[pl.BlockSpec(memory_space=pltpu.HBM)] * 3,
+            pltpu.VMEM((rows, width), jnp.bfloat16),
+        ],
+        in_specs=[pl.BlockSpec(memory_space=pltpu.SMEM)] + [pl.BlockSpec(memory_space=pltpu.HBM)] * 3,
         out_specs=[pl.BlockSpec(memory_space=pltpu.VMEM)] * 2,
         scratch_shapes=[
             pltpu.VMEM(feed_pairs.shape[::-1], jnp.int32),
@@ -193,26 +201,35 @@
             pltpu.SemaphoreType.DMA((3,)),
         ],
         cost_estimate=pl.CostEstimate(
-            flops=2 * 2 * rows * 48 * 128, bytes_accessed=2 * SECOND_ROWS * width + 8 * rows, transcendentals=0
+            flops=2 * 2 * rows * 48 * 128, bytes_accessed=2 * rows * width + 8 * rows, transcendentals=0
         ),
         compiler_params=pltpu.CompilerParams(vmem_limit_bytes=16 * MIB),
         name="factors",
     )(
+        slot.reshape(1),
         *(
             pltpu.with_memory_space_constraint(given, pltpu.HBM)
             for given in (jnp.transpose(feed_pairs), feed_gains, beam)
+        ),
+    )
+
+
+def project_kernel(
+    spans, share_order, eager, got_ref, factor_ref, first_ref, second_ref, beam_ref, out_ref, late_ref, partial, sems
+):
+    rows = first_ref.shape[0]
+    late = [
+        pltpu.make_async_copy(
+            beam_ref.at[pl.ds(rows + start, size), :], late_ref.at[pl.ds(start, size), :], sems.at[group]
         )
-    )
-
-
-def project_kernel(spans, share_order, got_ref, factor_ref, first_ref, second_ref, beam_ref, out_ref, last_ref, sem):
-    places = []
-    begin = 0
-    for ref in (first_ref, second_ref, last_ref):
-        places.append((begin, ref))
-        begin += ref.shape[0]
-    late = pltpu.make_async_copy(beam_ref.at[pl.ds(places[-1][0], last_ref.shape[0]), :], last_ref, sem)
-    late.start()
+        for group, (start, size) in enumerate(spans)
+    ]
+
+    @pl.when(jnp.logical_not(eager))
+    def start_late():
+        for copy in late:
+            copy.start()
+
     total = got_ref[0].astype(jnp.float32)
     for source in range(1, got_ref.shape[0]):
         total += got_ref[source].astype(jnp.float32)
@@ -223,27 +240,33 @@
     rows16 = jnp.concatenate([high.astype(jnp.float32), low.astype(jnp.float32)], axis=0)
     row_group = jnp.bitwise_and(lax.broadcasted_iota(jnp.int32, rows16.shape, 0), GROUPS - 1)
     lefts = [jnp.where(row_group == group, rows16, 0.0).astype(jnp.bfloat16) for group in range(GROUPS)]
-    sums = []
-    waited = False
-    for part in range(2):
+
+    def products(ref, copies):
         value = None
         for group, (start, size) in enumerate(spans):
-            row = part * (spans[-1][0] + spans[-1][1]) + start
-            for begin, ref in places:
-                low = max(row, begin)
-                count = min(row + size, begin + ref.shape[0]) - low
-                if count <= 0:
-                    continue
-                if ref is last_ref and not waited:
-                    late.wait()
-                    waited = True
-                left = lefts[group][:, low - row:low - row + count]
-                term = jnp.dot(left, ref[pl.ds(low - begin, count), :], preferred_element_type=jnp.float32)
-                value = term if value is None else value + term
+            if copies:
+                copies[group].wait()
+            term = jnp.dot(
+                lefts[group][:, :size], ref[pl.ds(start, size), :], preferred_element_type=jnp.float32
+            )
+            value = term if value is None else value + term
+        return value
+
+    def collected(value):
         value = value[:2 * GROUPS] + value[2 * GROUPS:]
-        sums.append(
-            [jnp.sum(value[piece * GROUPS:(piece + 1) * GROUPS], axis=0, keepdims=True) for piece in range(2)]
-        )
+        return [jnp.sum(value[piece * GROUPS:(piece + 1) * GROUPS], axis=0, keepdims=True) for piece in range(2)]
+
+    sums = [collected(products(first_ref, None))]
+
+    @pl.when(eager)
+    def use_early():
+        partial[...] = products(second_ref, None)
+
+    @pl.when(jnp.logical_not(eager))
+    def use_late():
+        partial[...] = products(late_ref, late)
+
+    sums.append(collected(partial[...]))
     answer = jnp.concatenate([sums[0][0] + sums[1][1], sums[0][1] - sums[1][0]], axis=0)
     width = answer.shape[1]
     share = width // len(share_order)
@@ -251,22 +274,29 @@
         out_ref[slab, :, :share] = answer[:, k * share:(k + 1) * share]
 
 
-def project(got, factor, first, second, beam, share_order):
+def project(got, factor, first, second, beam, share_order, slot, eager_slots):
     rows, width = beam.shape
     spans = group_spans(rows // 2)
 
-    def body(*refs):
-        project_kernel(spans, share_order, *refs)
+    def body(slot_ref, *refs):
+        project_kernel(spans, share_order, slot_ref[0] < eager_slots, *refs)
 
     return pl.pallas_call(
         body,
         out_shape=jax.ShapeDtypeStruct((len(share_order), 2, padded(width // len(share_order))), jnp.float32),
-        in_specs=[pl.BlockSpec(memory_space=pltpu.VMEM)] * 4 + [pl.BlockSpec(memory_space=pltpu.HBM)],
+        in_specs=[pl.BlockSpec(memory_space=pltpu.SMEM)]
+        + [pl.BlockSpec(memory_space=pltpu.VMEM)] * 4
+        + [pl.BlockSpec(memory_space=pltpu.HBM)],
         out_specs=pl.BlockSpec(memory_space=pltpu.VMEM),
-        scratch_shapes=[pltpu.VMEM((rows - FIRST_ROWS - SECOND_ROWS, width), jnp.bfloat16), pltpu.SemaphoreType.DMA],
+        scratch_shapes=[
+            pltpu.VMEM((rows // 2, width), jnp.bfloat16),
+            pltpu.VMEM((4 * GROUPS, width), jnp.float32),
+            pltpu.SemaphoreType.DMA((GROUPS,)),
+        ],
         compiler_params=pltpu.CompilerParams(vmem_limit_bytes=16 * MIB),
         name="project",
     )(
+        slot.reshape(1),
         *(pltpu.with_memory_space_constraint(held, pltpu.VMEM) for held in (got, factor, first, second)),
         pltpu.with_memory_space_constraint(beam, pltpu.HBM),
     )
@@ -278,15 +308,16 @@
     share_width = beam_blocks.shape[3] // shares
     order = rotated(slots // 2, slots // 4)
     beam = beam_blocks.reshape(2 * beam_blocks.shape[2], beam_blocks.shape[3])
-    keep, send, first = transform(visibilities, beam, m_order, lax.axis_index("ma"), order)
+    slot = lax.axis_index("ma")
+    keep, send, first = transform(visibilities, beam, m_order, slot, order)
     send, feed_gains = lax.optimization_barrier((send, feed_gains))
-    factor, second = factors(feed_pairs, feed_gains, beam)
+    factor, second = factors(feed_pairs, feed_gains, beam, slot, slots // 2)
     other = lax.ppermute(send, "ma", [(slot, slot ^ 1) for slot in range(slots)])
     pair, factor = lax.optimization_barrier(((keep + other).astype(jnp.bfloat16), factor))
     same_core = [[2 * i + parity for i in order] for parity in range(2)]
     got = lax.all_to_all(pair, "ma", split_axis=0, concat_axis=0, tiled=True, axis_index_groups=same_core)
     share_order = rotated(shares, shares // 2 + 1)
-    partial_modes = project(got, factor, first, second, beam, share_order)
+    partial_modes = project(got, factor, first, second, beam, share_order, slot, slots // 2)
     parts = lax.all_to_all(
         partial_modes, "bl", split_axis=0, concat_axis=0, tiled=True, axis_index_groups=[share_order]
     )

time: 34.8 us -> 34 us (0.977)
  blocking collectives: 27.3 us -> 26.2 us
    all_to_all x1, blocking collectives: 17.1 us -> 16.1 us  [per_device(): lax.all_to_all(pair, 'ma', split_axis=0, concat_axis=0, tiled=True, axis_...]
  transfers between devices with their start and end apart: 1 -> 1, of which waited for: 0 -> 0; matrix products, arithmetic and copies ran while one was open for 0% -> 0% of each run, Pallas kernels for 6% -> 7%
where the time goes in v5:
time: 34 us; the launch traced here: 33.7 us
  blocking collectives  26.2 us (77%)
  Pallas kernels  6.7 us (20%)
  other arithmetic  0.61 us (2%)
    all_to_all x1, blocking collectives, per_device(): lax.all_to_all(pair, 'ma', split_axis=0, concat_axis=0, tiled=True, axis_...  16.1 us
    all_to_all x1, blocking collectives, per_device(): lax.all_to_all(partial_modes, 'bl', split_axis=0, concat_axis=0, tiled=Tr...  10.2 us
    pallas_call x1, Pallas kernels, transform(): pl.pallas_call(body, out_shape=[pltpu.VMEM((count // 2, 2 * GROUPS, width...  2.92 us
    pallas_call x1, Pallas kernels, factors(): pl.pallas_call(body, out_shape=[pltpu.VMEM((2, 2 * GROUPS, line), jnp.flo...  2.27 us
    pallas_call x1, Pallas kernels, project(): pl.pallas_call(body, out_shape=jax.ShapeDtypeStruct((len(share_order), 2,...  1.51 us
  transfers between devices with their start and end apart: 1, of which 0 were waited for; matrix products, arithmetic and copies ran while one was open for 0% of the time, Pallas kernels for 7%

profile of v5, /device:TPU:8, one launch (start us, length us, event | category | flops | bytes accessed | tf_op | source)
XLA Modules:
  0.0 33.7 jit_solution(9767315006145843966)
XLA Ops:
  0.0 2.9 %transform.1 = (f32[16,8,640]{2,1,0:T(8,128)S(1)}, f32[16,8,640]{2,1,0:T(8,128)S(1)}, bf16[2080,1000]{1,0:T(8,128)(2,1)S(1)}) custom-call(s32[1]{0:T(128)} %bitcast.slot_ref, s32[32]{0:T(128)} %refs_0_.1, bf16[2,2080,256]{2,1,0:T(8,128)(2,1)} %refs_1_.1, bf16[4160,1000]{1,0:T(8,128)(2,1)} %bitcast.5), custom_call_target="tpu_custom_call" | custom-call | tf_op jit(solution)/shard_map/transform/pallas_call | solution.py:98
  2.9 0.1 collective-permute-start
  3.0 2.3 %factors.1 = (f32[2,8,640]{2,1,0:T(8,128)S(1)}, bf16[2080,1000]{1,0:T(8,128)(2,1)S(1)}) custom-call(s32[1]{0:T(128)} %bitcast.slot_ref, s32[2,2080]{1,0:T(2,128)} %bitcast.8, f32[2,1024]{1,0:T(2,128)} %refs_1_.2, bf16[4160,1000]{1,0:T(8,128)(2,1)} %bitcast.6), custom_call_target="tpu_custom_call" | custom-call | flops 51118080 | bytes 4176640 | tf_op jit(solution)/shard_map/factors/pallas_call | solution.py:190
  5.3 0.0 collective-permute-done
  5.4 16.1 %all_to_all.10.refs_0_ = bf16[16,8,640]{2,1,0:T(8,128)(2,1)S(1)} all-to-all(bf16[16,8,640]{2,1,0:T(8,128)(2,1)S(1)} %add_convert_fusion), channel_id=1, replica_groups={{128,144,160,176,192,208,224,240,0,16,32,48,64,80,96,112},{136,152,168,..., dimensions={0} | all-to-all | bytes 327680 | tf_op jit(solution)/shard_map/all_to_all | solution.py:318
  21.4 1.5 %project.1 = f32[8,2,128]{2,1,0:T(2,128)S(1)} custom-call(s32[1]{0:T(128)} %bitcast.slot_ref, bf16[16,8,640]{2,1,0:T(8,128)(2,1)S(1)} %all_to_all.10.refs_0_, f32[2,8,640]{2,1,0:T(8,128)S(1)} %get-tuple-element.20.refs_1_, bf16[2080,1000]{1,0:T(8,128)(2,1)S(1)} %get-tuple-element.21.refs_2_, bf16[2080,1000]{1,0:T(8,128)(2,1)S(1)} %get-tuple-element.22.refs_3_, ...), custom_call_target="tpu_custom_call" | custom-call | tf_op jit(solution)/shard_map/project/pallas_call | solution.py:284
  22.9 10.2 %all_to_all.11 = f32[8,2,128]{2,1,0:T(2,128)S(1)} all-to-all(f32[8,2,128]{2,1,0:T(2,128)S(1)} %project.1), channel_id=1, replica_groups={{5,6,7,0,1,2,3,4},{13,14,15,8,9,10,11,12},{21,22,23,16,17,18,19,20},{29..., dimensions={0} | all-to-all | bytes 16384 | tf_op jit(solution)/shard_map/all_to_all | solution.py:321
  33.1 0.6 %reduce_sum.9 = f32[2,128]{1,0:T(2,128)} reduce(f32[8,2,128]{2,1,0:T(2,128)S(1)} %all_to_all.11, f32[]{:T(128)} %constant.7.clone.1), dimensions={0}, to_apply=%region_0.0 | reduce | flops 1792 | bytes 9220 | tf_op jit(solution)/shard_map/reduce_sum | solution.py:324
  (1 shorter events, 0.0 us)
Async XLA Ops:
  2.9 2.4 %collective-permute-start = (f32[16,8,640]{2,1,0:T(8,128)S(1)}, f32[16,8,640]{2,1,0:T(8,128)S(1)}, u32[]{:S(2)}, u32[]{:S(2)}) collective-permute-start(f32[16,8,640]{2,1,0:T(8,128)S(1)} %get-tuple-element.16), channel_id=1, source_target_pairs={{0,8},{8,0},{16,24},{24,16},{32,40},{40,32},{48,56},{56,48},{64,72... | collective-permute-start | bytes 983048 | tf_op jit(solution)/shard_map/ppermute | solution.py:315

commit v6 on v5

--- a/solution.py
+++ b/solution.py
@@ -82,7 +82,7 @@
     for piece in range(lines.shape[0]):
         block = lines[piece].reshape(count, 2 * GROUPS, LANES)
         keep_ref[:, :, piece * LANES:(piece + 1) * LANES] = block[:half]
-        send_ref[:, :, piece * LANES:(piece + 1) * LANES] = block[half:]
+        send_ref[:, :, piece * LANES:(piece + 1) * LANES] = block[half:].astype(jnp.bfloat16)
     early.wait()
 
 
@@ -97,7 +97,7 @@
 
     return pl.pallas_call(
         body,
-        out_shape=[pltpu.VMEM((count // 2, 2 * GROUPS, width), jnp.float32)] * 2
+        out_shape=[pltpu.VMEM((count // 2, 2 * GROUPS, width), kind) for kind in (jnp.float32, jnp.bfloat16)]
         + [pltpu.VMEM((beam.shape[0] // 2, beam.shape[1]), jnp.bfloat16)],
         in_specs=[
             pl.BlockSpec(memory_space=pltpu.SMEM),
@@ -313,7 +313,7 @@
     send, feed_gains = lax.optimization_barrier((send, feed_gains))
     factor, second = factors(feed_pairs, feed_gains, beam, slot, slots // 2)
     other = lax.ppermute(send, "ma", [(slot, slot ^ 1) for slot in range(slots)])
-    pair, factor = lax.optimization_barrier(((keep + other).astype(jnp.bfloat16), factor))
+    pair, factor = lax.optimization_barrier(((keep + other.astype(jnp.float32)).astype(jnp.bfloat16), factor))
     same_core = [[2 * i + parity for i in order] for parity in range(2)]
     got = lax.all_to_all(pair, "ma", split_axis=0, concat_axis=0, tiled=True, axis_index_groups=same_core)
     share_order = rotated(shares, shares // 2 + 1)

time: 34 us -> 33.8 us (level)
  no operation moved by 1% of the time
where the time goes in v6:
time: 33.8 us; the launch traced here: 33.5 us
  blocking collectives  26.1 us (77%)
  Pallas kernels  6.7 us (20%)
  other arithmetic  0.61 us (2%)
    all_to_all x1, blocking collectives, per_device(): lax.all_to_all(pair, 'ma', split_axis=0, concat_axis=0, tiled=True, axis_...  15.9 us
    all_to_all x1, blocking collectives, per_device(): lax.all_to_all(partial_modes, 'bl', split_axis=0, concat_axis=0, tiled=Tr...  10.2 us
    pallas_call x1, Pallas kernels, transform(): pl.pallas_call(body, out_shape=[pltpu.VMEM((count // 2, 2 * GROUPS, width...  2.92 us
    pallas_call x1, Pallas kernels, factors(): pl.pallas_call(body, out_shape=[pltpu.VMEM((2, 2 * GROUPS, line), jnp.flo...  2.27 us
    pallas_call x1, Pallas kernels, project(): pl.pallas_call(body, out_shape=jax.ShapeDtypeStruct((len(share_order), 2,...  1.51 us
  transfers between devices with their start and end apart: 1, of which 0 were waited for; matrix products, arithmetic and copies ran while one was open for 0% of the time, Pallas kernels for 7%

profile of v6, /device:TPU:8, one launch (start us, length us, event | category | flops | bytes accessed | tf_op | source)
XLA Modules:
  0.0 33.5 jit_solution(3221782920012227722)
XLA Ops:
  0.0 2.9 %transform.1 = (f32[16,8,640]{2,1,0:T(8,128)S(1)}, bf16[16,8,640]{2,1,0:T(8,128)(2,1)S(1)}, bf16[2080,1000]{1,0:T(8,128)(2,1)S(1)}) custom-call(s32[1]{0:T(128)} %bitcast.slot_ref, s32[32]{0:T(128)} %refs_0_.1, bf16[2,2080,256]{2,1,0:T(8,128)(2,1)} %refs_1_.1, bf16[4160,1000]{1,0:T(8,128)(2,1)} %bitcast.5), custom_call_target="tpu_custom_call" | custom-call | tf_op jit(solution)/shard_map/transform/pallas_call | solution.py:98
  2.9 0.1 collective-permute-start
  3.0 2.3 %factors.1 = (f32[2,8,640]{2,1,0:T(8,128)S(1)}, bf16[2080,1000]{1,0:T(8,128)(2,1)S(1)}) custom-call(s32[1]{0:T(128)} %bitcast.slot_ref, s32[2,2080]{1,0:T(2,128)} %bitcast.8, f32[2,1024]{1,0:T(2,128)} %refs_1_.2, bf16[4160,1000]{1,0:T(8,128)(2,1)} %bitcast.6), custom_call_target="tpu_custom_call" | custom-call | flops 51118080 | bytes 4176640 | tf_op jit(solution)/shard_map/factors/pallas_call | solution.py:190
  5.3 0.0 collective-permute-done
  5.4 15.9 %all_to_all.10.refs_0_ = bf16[16,8,640]{2,1,0:T(8,128)(2,1)S(1)} all-to-all(bf16[16,8,640]{2,1,0:T(8,128)(2,1)S(1)} %add_convert_fusion), channel_id=1, replica_groups={{128,144,160,176,192,208,224,240,0,16,32,48,64,80,96,112},{136,152,168,..., dimensions={0} | all-to-all | bytes 327680 | tf_op jit(solution)/shard_map/all_to_all | solution.py:318
  21.3 1.5 %project.1 = f32[8,2,128]{2,1,0:T(2,128)S(1)} custom-call(s32[1]{0:T(128)} %bitcast.slot_ref, bf16[16,8,640]{2,1,0:T(8,128)(2,1)S(1)} %all_to_all.10.refs_0_, f32[2,8,640]{2,1,0:T(8,128)S(1)} %get-tuple-element.20.refs_1_, bf16[2080,1000]{1,0:T(8,128)(2,1)S(1)} %get-tuple-element.21.refs_2_, bf16[2080,1000]{1,0:T(8,128)(2,1)S(1)} %get-tuple-element.22.refs_3_, ...), custom_call_target="tpu_custom_call" | custom-call | tf_op jit(solution)/shard_map/project/pallas_call | solution.py:284
  22.8 10.2 %all_to_all.11 = f32[8,2,128]{2,1,0:T(2,128)S(1)} all-to-all(f32[8,2,128]{2,1,0:T(2,128)S(1)} %project.1), channel_id=1, replica_groups={{5,6,7,0,1,2,3,4},{13,14,15,8,9,10,11,12},{21,22,23,16,17,18,19,20},{29..., dimensions={0} | all-to-all | bytes 16384 | tf_op jit(solution)/shard_map/all_to_all | solution.py:321
  33.0 0.6 %reduce_sum.9 = f32[2,128]{1,0:T(2,128)} reduce(f32[8,2,128]{2,1,0:T(2,128)S(1)} %all_to_all.11, f32[]{:T(128)} %constant.7.clone.1), dimensions={0}, to_apply=%region_0.0 | reduce | flops 1792 | bytes 9220 | tf_op jit(solution)/shard_map/reduce_sum | solution.py:324
  (1 shorter events, 0.0 us)
Async XLA Ops:
  2.9 2.4 %collective-permute-start = (bf16[16,8,640]{2,1,0:T(8,128)(2,1)S(1)}, bf16[16,8,640]{2,1,0:T(8,128)(2,1)S(1)}, u32[]{:S(2)}, u32[]{:S(2)}) collective-permute-start(bf16[16,8,640]{2,1,0:T(8,128)(2,1)S(1)} %get-tuple-element.16), channel_id=1, source_target_pairs={{0,8},{8,0},{16,24},{24,16},{32,40},{40,32},{48,56},{56,48},{64,72... | collective-permute-start | bytes 491528 | tf_op jit(solution)/shard_map/ppermute | solution.py:315

commit v7 on v6

--- a/solution.py
+++ b/solution.py
@@ -73,16 +73,19 @@
         found += lax.dot_general(for_imag, held[1, rows, :], contract, preferred_element_type=jnp.float32)
         for piece, (at, width) in enumerate(lane_pieces(lines.shape[0] * LANES)):
             for part in range(2):
-                to = pl.ds(part * GROUPS + group, count, stride=2 * GROUPS)
+                to = pl.ds(part * GROUPS + group, half, stride=2 * GROUPS)
                 filled = min(width, max(size - at, 0))
+                kept = slice(part * count, part * count + half)
+                sent = slice(part * count + half, (part + 1) * count)
                 if filled < width:
-                    lines[piece, to, :] = jnp.zeros((count, width), jnp.float32)
+                    lines[piece, to, :] = jnp.zeros((half, width), jnp.float32)
+                    keep_ref[:, part * GROUPS + group, at:at + width] = jnp.zeros((half, width), jnp.float32)
                 if filled > 0:
-                    lines[piece, to, :filled] = found[part * count:(part + 1) * count, at:at + filled]
+                    lines[piece, to, :filled] = found[sent, at:at + filled]
+                    keep_ref[:, part * GROUPS + group, at:at + filled] = found[kept, at:at + filled]
     for piece in range(lines.shape[0]):
-        block = lines[piece].reshape(count, 2 * GROUPS, LANES)
-        keep_ref[:, :, piece * LANES:(piece + 1) * LANES] = block[:half]
-        send_ref[:, :, piece * LANES:(piece + 1) * LANES] = block[half:].astype(jnp.bfloat16)
+        block = lines[piece].reshape(half, 2 * GROUPS, LANES)
+        send_ref[:, :, piece * LANES:(piece + 1) * LANES] = block.astype(jnp.bfloat16)
     early.wait()
 
 
@@ -108,7 +111,7 @@
         out_specs=[pl.BlockSpec(memory_space=pltpu.VMEM)] * 3,
         scratch_shapes=[
             pltpu.VMEM((2, rows, times), jnp.bfloat16),
-            pltpu.VMEM((width // LANES, count * 2 * GROUPS, LANES), jnp.float32),
+            pltpu.VMEM((width // LANES, count // 2 * 2 * GROUPS, LANES), jnp.float32),
             pltpu.SMEM((count,), jnp.int32),
             pltpu.SemaphoreType.DMA((GROUPS + 2,)),
         ],

time: 33.8 us -> 33.8 us (level)
  no operation moved by 1% of the time
where the time goes in v7:
time: 33.8 us; the launch traced here: 33.5 us
  blocking collectives  26.1 us (77%)
  Pallas kernels  6.7 us (20%)
  other arithmetic  0.61 us (2%)
    all_to_all x1, blocking collectives, per_device(): lax.all_to_all(pair, 'ma', split_axis=0, concat_axis=0, tiled=True, axis_...  15.9 us
    all_to_all x1, blocking collectives, per_device(): lax.all_to_all(partial_modes, 'bl', split_axis=0, concat_axis=0, tiled=Tr...  10.2 us
    pallas_call x1, Pallas kernels, transform(): pl.pallas_call(body, out_shape=[pltpu.VMEM((count // 2, 2 * GROUPS, width...  2.92 us
    pallas_call x1, Pallas kernels, factors(): pl.pallas_call(body, out_shape=[pltpu.VMEM((2, 2 * GROUPS, line), jnp.flo...  2.27 us
    pallas_call x1, Pallas kernels, project(): pl.pallas_call(body, out_shape=jax.ShapeDtypeStruct((len(share_order), 2,...  1.51 us
  transfers between devices with their start and end apart: 1, of which 0 were waited for; matrix products, arithmetic and copies ran while one was open for 0% of the time, Pallas kernels for 7%

profile of v7, /device:TPU:8, one launch (start us, length us, event | category | flops | bytes accessed | tf_op | source)
XLA Modules:
  0.0 33.5 jit_solution(9051722031686834041)
XLA Ops:
  0.0 2.9 %transform.1 = (f32[16,8,640]{2,1,0:T(8,128)S(1)}, bf16[16,8,640]{2,1,0:T(8,128)(2,1)S(1)}, bf16[2080,1000]{1,0:T(8,128)(2,1)S(1)}) custom-call(s32[1]{0:T(128)} %bitcast.slot_ref, s32[32]{0:T(128)} %refs_0_.1, bf16[2,2080,256]{2,1,0:T(8,128)(2,1)} %refs_1_.1, bf16[4160,1000]{1,0:T(8,128)(2,1)} %bitcast.5), custom_call_target="tpu_custom_call" | custom-call | tf_op jit(solution)/shard_map/transform/pallas_call | solution.py:101
  2.9 0.1 collective-permute-start
  3.0 2.3 %factors.1 = (f32[2,8,640]{2,1,0:T(8,128)S(1)}, bf16[2080,1000]{1,0:T(8,128)(2,1)S(1)}) custom-call(s32[1]{0:T(128)} %bitcast.slot_ref, s32[2,2080]{1,0:T(2,128)} %bitcast.8, f32[2,1024]{1,0:T(2,128)} %refs_1_.2, bf16[4160,1000]{1,0:T(8,128)(2,1)} %bitcast.6), custom_call_target="tpu_custom_call" | custom-call | flops 51118080 | bytes 4176640 | tf_op jit(solution)/shard_map/factors/pallas_call | solution.py:193
  5.3 0.0 collective-permute-done
  5.4 15.9 %all_to_all.10.refs_0_ = bf16[16,8,640]{2,1,0:T(8,128)(2,1)S(1)} all-to-all(bf16[16,8,640]{2,1,0:T(8,128)(2,1)S(1)} %add_convert_fusion), channel_id=1, replica_groups={{128,144,160,176,192,208,224,240,0,16,32,48,64,80,96,112},{136,152,168,..., dimensions={0} | all-to-all | bytes 327680 | tf_op jit(solution)/shard_map/all_to_all | solution.py:321
  21.3 1.5 %project.1 = f32[8,2,128]{2,1,0:T(2,128)S(1)} custom-call(s32[1]{0:T(128)} %bitcast.slot_ref, bf16[16,8,640]{2,1,0:T(8,128)(2,1)S(1)} %all_to_all.10.refs_0_, f32[2,8,640]{2,1,0:T(8,128)S(1)} %get-tuple-element.20.refs_1_, bf16[2080,1000]{1,0:T(8,128)(2,1)S(1)} %get-tuple-element.21.refs_2_, bf16[2080,1000]{1,0:T(8,128)(2,1)S(1)} %get-tuple-element.22.refs_3_, ...), custom_call_target="tpu_custom_call" | custom-call | tf_op jit(solution)/shard_map/project/pallas_call | solution.py:287
  22.8 10.2 %all_to_all.11 = f32[8,2,128]{2,1,0:T(2,128)S(1)} all-to-all(f32[8,2,128]{2,1,0:T(2,128)S(1)} %project.1), channel_id=1, replica_groups={{5,6,7,0,1,2,3,4},{13,14,15,8,9,10,11,12},{21,22,23,16,17,18,19,20},{29..., dimensions={0} | all-to-all | bytes 16384 | tf_op jit(solution)/shard_map/all_to_all | solution.py:324
  33.0 0.6 %reduce_sum.9 = f32[2,128]{1,0:T(2,128)} reduce(f32[8,2,128]{2,1,0:T(2,128)S(1)} %all_to_all.11, f32[]{:T(128)} %constant.7.clone.1), dimensions={0}, to_apply=%region_0.0 | reduce | flops 1792 | bytes 9220 | tf_op jit(solution)/shard_map/reduce_sum | solution.py:327
  (1 shorter events, 0.0 us)
Async XLA Ops:
  2.9 2.4 %collective-permute-start = (bf16[16,8,640]{2,1,0:T(8,128)(2,1)S(1)}, bf16[16,8,640]{2,1,0:T(8,128)(2,1)S(1)}, u32[]{:S(2)}, u32[]{:S(2)}) collective-permute-start(bf16[16,8,640]{2,1,0:T(8,128)(2,1)S(1)} %get-tuple-element.16), channel_id=1, source_target_pairs={{0,8},{8,0},{16,24},{24,16},{32,40},{40,32},{48,56},{56,48},{64,72... | collective-permute-start | bytes 491528 | tf_op jit(solution)/shard_map/ppermute | solution.py:318
